TPU v7x, 32 devices: a whole 2x2x4 slice. The times are simulated.
32 devices in a mesh: groups: 2 (over y), seq: 8 (over z, x), heads: 2 (over core).
Axes of the slice: x: 2, y: 2, z: 4, core: 2. Of those that a mesh axis runs over, the one named last changes fastest.
Arguments:
- queries: bfloat16 [8192, 16, 128], P(('groups', 'seq'), 'heads'), parts along dimension 0, may hold values from -128 to 128
- keys: bfloat16 [8192, 16, 128], P(('groups', 'seq'), 'heads'), parts along dimension 0, may hold values from -128 to 128
- values: bfloat16 [8192, 16, 128], P(('groups', 'seq'), 'heads'), parts along dimension 0, may hold values from -6 to 6
Outputs:
- attended: bfloat16 [8192, 16, 128], P(('groups', 'seq'), 'heads'), parts along dimension 0
There are 2 independent parts, one for each index of `groups`. A program takes and returns all parts, laid end to end along the dimension named above; each array names one. Nothing has to cross between parts.
All inputs are finite; a program needn't handle non-finite values.
Results may differ from a plain program's by a relative error of at most 0.0055.
Values may be sent and summed in bfloat16 or wider, within the bound.
No kernel may reach another device: no remote copies, remote signals or barrier semaphores. Data moves between devices by JAX's collectives and lax.ppermute only.
A program may use at most 128 MiB of HBM per device.

v0:
```python
import math

import jax
import jax.numpy as jnp
from jax import lax
from jax.sharding import PartitionSpec as P

BLOCK = 64


neg_big = -1e30
log_two = math.log(2.0)
sectioned_rows = 512


def passed_along(value, axis, steps):
    count = lax.axis_size(axis)
    initial, last = (max(0, -steps), min(count, count - steps))
    return lax.ppermute(value, axis, [(source, source + steps) for source in range(initial, last)])


def pool_rows(block, factor):
    count = block.shape[0] // factor
    grouped = block.astype(jnp.float32).reshape(count, factor, block.shape[1], block.shape[2])
    return jnp.mean(grouped, axis=1).astype(jnp.bfloat16)


def level_scores(query_block, key_rows, valid, bias, scale):
    scores = jnp.einsum("qhd,khd->hqk", query_block, key_rows, preferred_element_type=jnp.float32)
    return jnp.where(valid[None], scores * scale + bias, neg_big)


def shards(queries, keys, values):
    rows, heads, width = queries.shape
    quad = 4 * BLOCK
    scale = 1.0 / math.sqrt(width)
    first = lax.axis_index("seq") * rows
    own1_k = pool_rows(keys, 2)
    own1_v = pool_rows(values, 2)
    own2_k = pool_rows(keys, 4)
    own2_v = pool_rows(values, 4)
    tail_k, tail_v = passed_along((keys[rows - quad :], values[rows - quad :]), "seq", 1)
    lead = (
        tail_k[quad - BLOCK :],
        tail_v[quad - BLOCK :],
        pool_rows(tail_k[quad - 2 * BLOCK :], 2),
        pool_rows(tail_v[quad - 2 * BLOCK :], 2),
        pool_rows(tail_k, 4),
        pool_rows(tail_v, 4),
    )
    ext0_k = jnp.concatenate([lead[0], keys], 0)
    ext0_v = jnp.concatenate([lead[1], values], 0)
    ext1_k = jnp.concatenate([lead[2], own1_k], 0)
    ext1_v = jnp.concatenate([lead[3], own1_v], 0)
    ext2_k = jnp.concatenate([lead[4], own2_k], 0)
    ext2_v = jnp.concatenate([lead[5], own2_v], 0)

    def one_block(blk):
        local = blk * quad
        start = first + local
        posit = start + jnp.arange(quad, dtype=jnp.int32)
        bound0 = (posit // BLOCK - 1) * BLOCK
        bound1 = (posit // (2 * BLOCK) - 1) * 2 * BLOCK
        bound2 = (posit // quad - 1) * quad
        query_block = lax.dynamic_slice_in_dim(queries, local, quad, 0)
        tokens0 = start - BLOCK + jnp.arange(quad + BLOCK, dtype=jnp.int32)
        rows1 = start // 2 - BLOCK + jnp.arange(quad // 2 + BLOCK, dtype=jnp.int32)
        rows2 = start // 4 - BLOCK + jnp.arange(quad // 4 + BLOCK, dtype=jnp.int32)
        key0 = lax.dynamic_slice_in_dim(ext0_k, local, quad + BLOCK, 0)
        val0 = lax.dynamic_slice_in_dim(ext0_v, local, quad + BLOCK, 0)
        key1 = lax.dynamic_slice_in_dim(ext1_k, local // 2, quad // 2 + BLOCK, 0)
        val1 = lax.dynamic_slice_in_dim(ext1_v, local // 2, quad // 2 + BLOCK, 0)
        key2 = lax.dynamic_slice_in_dim(ext2_k, local // 4, quad // 4 + BLOCK, 0)
        val2 = lax.dynamic_slice_in_dim(ext2_v, local // 4, quad // 4 + BLOCK, 0)
        valid0 = (
            (tokens0 >= 0)[None]
            & (tokens0[None] >= bound0[:, None])
            & (tokens0[None] <= posit[:, None])
        )
        valid1 = (
            (rows1 >= 0)[None]
            & (2 * rows1[None] >= bound1[:, None])
            & (2 * rows1[None] + 2 <= bound0[:, None])
        )
        valid2 = (
            (rows2 >= 0)[None]
            & (4 * rows2[None] >= bound2[:, None])
            & (4 * rows2[None] + 4 <= bound1[:, None])
        )
        scores = jnp.concatenate(
            [
                level_scores(query_block, key0, valid0, 0.0, scale),
                level_scores(query_block, key1, valid1, log_two, scale),
                level_scores(query_block, key2, valid2, 2.0 * log_two, scale),
            ],
            axis=2,
        )
        value_rows = jnp.concatenate([val0, val1, val2], 0)
        top = jnp.max(scores, axis=2)
        weights = jnp.exp(scores - top[..., None])
        total = jnp.sum(weights, axis=2)
        summed = jnp.einsum(
            "hqk,khd->hqd",
            weights.astype(jnp.bfloat16),
            value_rows,
            preferred_element_type=jnp.float32,
        )
        return (top, total, summed)

    tops, totals, sums = lax.map(one_block, jnp.arange(rows // quad, dtype=jnp.int32))
    top = tops.transpose(1, 0, 2).reshape(heads, rows)
    total = totals.transpose(1, 0, 2).reshape(heads, rows)
    summed = sums.transpose(1, 0, 2, 3).reshape(heads, rows, width)
    positions = first + jnp.arange(rows, dtype=jnp.int32)
    bound_far = (positions // quad - 1) * quad
    bound_last = bound_far[rows - 1]
    beyond = rows * lax.axis_size("seq")
    coarse_k = pool_rows(keys, 8)
    coarse_v = pool_rows(values, 8)

    def attend(inner, block_k, block_v, block_rows):

        def work(state):
            best, weight_sum, accum = state
            valid = 8 * block_rows[None] + 8 <= bound_far[:, None]
            scores = level_scores(queries, block_k, valid, 3.0 * log_two, scale)
            fresh = jnp.maximum(best, jnp.max(scores, axis=2))
            fade = jnp.exp(best - fresh)
            weights = jnp.exp(scores - fresh[..., None])
            weight_sum = weight_sum * fade + jnp.sum(weights, axis=2)
            accum = accum * fade[..., None] + jnp.einsum(
                "hqk,khd->hqd",
                weights.astype(jnp.bfloat16),
                block_v,
                preferred_element_type=jnp.float32,
            )
            return (fresh, weight_sum, accum)

        lowest = jnp.min(block_rows)
        return lax.cond(8 * lowest + 8 <= bound_last, work, lambda state: state, inner)

    def absorb(carry, piece):
        best, weight_sum, accum, section_k, section_v, section_rows, fill = carry
        piece_k, piece_v = piece
        count = piece_k.shape[0]
        piece_rows = jnp.arange(count, dtype=jnp.int32)
        if count > sectioned_rows:
            width_sub = max((size for size in range(1, sectioned_rows + 1) if count % size == 0))
            split_k = piece_k.reshape(count // width_sub, width_sub, heads, width)
            split_v = piece_v.reshape(count // width_sub, width_sub, heads, width)
            split_rows = piece_rows.reshape(count // width_sub, width_sub)

            def step(state, item):
                return (attend(state, item[0], item[1], item[2]), None)

            inner, unused = lax.scan(
                step, (best, weight_sum, accum), (split_k, split_v, split_rows)
            )
            best, weight_sum, accum = inner
            return (best, weight_sum, accum, section_k, section_v, section_rows, fill)
        section_k = lax.dynamic_update_slice_in_dim(section_k, piece_k, fill, 0)
        section_v = lax.dynamic_update_slice_in_dim(section_v, piece_v, fill, 0)
        section_rows = lax.dynamic_update_slice_in_dim(section_rows, piece_rows, fill, 0)
        fill = fill + count

        def flush(state):
            best, weight_sum, accum, section_k, section_v, section_rows, fill = state
            best, weight_sum, accum = attend(
                (best, weight_sum, accum),
                section_k[:sectioned_rows],
                section_v[:sectioned_rows],
                section_rows[:sectioned_rows],
            )
            blank = jnp.zeros((sectioned_rows, heads, width), jnp.bfloat16)
            section_k = jnp.concatenate([section_k[sectioned_rows:], blank], 0)
            section_v = jnp.concatenate([section_v[sectioned_rows:], blank], 0)
            section_rows = jnp.concatenate(
                [section_rows[sectioned_rows:], jnp.full((sectioned_rows,), beyond, jnp.int32)], 0
            )
            return (
                best,
                weight_sum,
                accum,
                section_k,
                section_v,
                section_rows,
                fill - sectioned_rows,
            )

        return lax.cond(
            fill >= sectioned_rows,
            flush,
            lambda state: state,
            (best, weight_sum, accum, section_k, section_v, section_rows, fill),
        )

    empty_section = jnp.zeros((2 * sectioned_rows, heads, width), jnp.bfloat16)
    section_init = jnp.full((2 * sectioned_rows,), beyond, jnp.int32)
    init = (
        top,
        total,
        summed,
        empty_section,
        empty_section,
        section_init,
        jnp.zeros((), jnp.int32),
    )
    result = absorb(
        init,
        (
            lax.all_gather(coarse_k, "seq", axis=0, tiled=True),
            lax.all_gather(coarse_v, "seq", axis=0, tiled=True),
        ),
    )
    top, total, summed, section_k, section_v, section_rows, fill = result
    top, total, summed = attend(
        (top, total, summed),
        section_k[:sectioned_rows],
        section_v[:sectioned_rows],
        section_rows[:sectioned_rows],
    )
    return (summed / total[..., None]).transpose(1, 0, 2).astype(jnp.bfloat16)


def solution(mesh):
    return jax.shard_map(
        shards,
        mesh=mesh,
        in_specs=(
            P(("groups", "seq"), "heads", None),
            P(("groups", "seq"), "heads", None),
            P(("groups", "seq"), "heads", None),
        ),
        out_specs=P(("groups", "seq"), "heads", None),
        check_vma=False,
    )
```

profile of v0, /device:TPU:16, one launch (start us, length us, event | category | flops | bytes accessed | tf_op | source)
XLA Modules:
  0.0 123.0 jit_solution(372660217673981330)
XLA Ops:
  6.5 1.6 %bitcast_reduce_fusion.2 = f32[64,8,128]{2,1,0:T(8,128)S(1)} fusion(bf16[512,8,128]{2,1,0:T(8,128)(2,1)} %param.10), kind=kLoop, calls=%fused_computation.105 | loop fusion | flops 983040 | bytes 1310720 | tf_op jit(solution)/shard_map/reduce_sum | solution.py:25
  8.8 1.4 %copy.39 = bf16[512,8,128]{2,0,1:T(8,128)(2,1)S(1)} copy(bf16[512,8,128]{2,1,0:T(8,128)(2,1)} %param.10) | data formatting | bytes 2097152 | tf_op args[1]
  11.1 3.5 %collective-permute-start = (bf16[256,8,128]{2,0,1:T(8,128)(2,1)}, bf16[256,8,128]{2,0,1:T(8,128)(2,1)}, u32[]{:S(2)}, u32[]{:S(2)}) collective-permute-start(bf16[256,8,128]{2,0,1:T(8,128)(2,1)} %slice.36), channel_id=1, source_target_pairs={{0,2},{2,4},{4,6},{6,8},{8,10},{10,12},{12,14},{1,3},{3,5},{5,7},{... | collective-permute-start | bytes 1572872 | tf_op jit(solution)/shard_map/ppermute | solution.py:19
  15.7 3.4 %collective-permute-start.1 = (bf16[256,8,128]{2,0,1:T(8,128)(2,1)}, bf16[256,8,128]{2,0,1:T(8,128)(2,1)}, u32[]{:S(2)}, u32[]{:S(2)}) collective-permute-start(bf16[256,8,128]{2,0,1:T(8,128)(2,1)} %slice.39), channel_id=1, source_target_pairs={{0,2},{2,4},{4,6},{6,8},{8,10},{10,12},{12,14},{1,3},{3,5},{5,7},{... | collective-permute-start | bytes 1572872 | tf_op jit(solution)/shard_map/ppermute | solution.py:19
  20.0 1.3 %bitcast_reduce_fusion.6 = f32[256,8,128]{2,1,0:T(8,128)} fusion(bf16[512,8,128]{2,1,0:T(8,128)(2,1)S(1)} %copy-done.3), kind=kLoop, calls=%fused_computation.109 | loop fusion | flops 786432 | bytes 2097152 | tf_op jit(solution)/shard_map/reduce_sum | solution.py:25
  23.5 2.2 %multiply_convert_fusion.1 = bf16[256,8,128]{2,1,0:T(8,128)(2,1)} fusion(f32[256,8,128]{2,1,0:T(8,128)} %bitcast_reduce_fusion.6), kind=kLoop, calls=%fused_computation.116 | loop fusion | flops 524288 | bytes 1572864 | tf_op jit(solution)/shard_map/convert_element_type | solution.py:25
  25.6 1.9 %multiply_convert_fusion.3 = bf16[128,8,128]{2,1,0:T(8,128)(2,1)} fusion(f32[128,8,128]{2,1,0:T(8,128)} %bitcast_reduce_fusion.5), kind=kLoop, calls=%fused_computation.123 | loop fusion | flops 262144 | bytes 786432 | tf_op jit(solution)/shard_map/convert_element_type | solution.py:25
  29.9 3.5 %collective-permute-done = bf16[256,8,128]{2,0,1:T(8,128)(2,1)} collective-permute-done((bf16[256,8,128]{2,0,1:T(8,128)(2,1)}, bf16[256,8,128]{2,0,1:T(8,128)(2,1)}, u32[]{:S(2)}, u32[]{:S(2)}) %collective-permute-start) | collective-permute-done | bytes 524320 | tf_op jit(solution)/shard_map/ppermute | solution.py:19
  35.4 16.3 %collective-permute-done.1 = bf16[256,8,128]{2,0,1:T(8,128)(2,1)} collective-permute-done((bf16[256,8,128]{2,0,1:T(8,128)(2,1)}, bf16[256,8,128]{2,0,1:T(8,128)(2,1)}, u32[]{:S(2)}, u32[]{:S(2)}) %collective-permute-start.1) | collective-permute-done | bytes 524320 | tf_op jit(solution)/shard_map/ppermute | solution.py:19
  57.4 1.8 %convert_reduce_fusion.1 = f32[64,8,128]{2,0,1:T(8,128)S(1)} fusion(bf16[64,4,8,128]{3,1,0,2:T(4,128)(2,1)} %bitcast.27), kind=kLoop, calls=%fused_computation.114 | loop fusion | flops 458752 | bytes 786432 | tf_op jit(solution)/shard_map/reduce_sum | solution.py:25
  59.3 1.7 %convert_reduce_fusion = f32[64,8,128]{2,0,1:T(8,128)S(1)} fusion(bf16[64,4,8,128]{3,1,0,2:T(4,128)(2,1)} %bitcast.29), kind=kLoop, calls=%fused_computation.113 | loop fusion | flops 458752 | bytes 786432 | tf_op jit(solution)/shard_map/reduce_sum | solution.py:25
  64.7 34.1 %while.17 = (s32[]{:T(128)}, f32[2,8,256]{2,1,0:T(8,128)}, f32[2,8,256]{2,1,0:T(8,128)}, f32[2,8,256,128]{3,2,1,0:T(8,128)}, s32[2]{0:T(128)S(1)}, /*index=5*/s3...) while((s32[]{:T(128)}, f32[2,8,256]{2,1,0:T(8,128)}, ...), condition=%wide.region_13.14_spmd, body=%wide.region_8.13_spmd.sunk | while | flops 690760192 | bytes 39908296 | solution.py:110
  68.5 2.2 %fusion.92 = (f32[8,256]{1,0:T(8,128)}, f32[8,256,192]{1,2,0:T(8,128)}) fusion(bf16[192,8,128]{2,1,0:T(8,128)(2,1)S(1)} %get-tuple-element.547, bf16[256,8,128]{2,1,0:T(8,128)(2,1)S(1)} %constant_dynamic-slice_fusion.11, pred[256,192]{0,1:T(8,128)(4,1)S(1)} %compare_and_fusion.8), kind=kOutput, calls=%fused_computation.145.clone.1 | convolution fusion | flops 102234112 | bytes 2547712 | tf_op jit(solution)/shard_map/while/body/eval_jaxpr/qhd,khd->hqk/dot_general | solution.py:29
  71.5 1.6 %fusion.89 = (f32[8,256]{1,0:T(8,128)S(1)}, f32[8,256,320]{1,2,0:T(8,128)S(1)}) fusion(bf16[576,8,128]{2,0,1:T(8,128)(2,1)} %get-tuple-element.613, s32[]{:T(128)S(6)} %select_n.192, bf16[256,8,128]{2,1,0:T(8,128)(2,1)S(1)} %constant_dynamic-slice_fusion.11, pred[256,320]{0,1:T(8,128)(4,1)} %compare_and_fusion.7), kind=kOutput, calls=%fused_computation.144.clone.1 | convolution fusion | flops 169736192 | bytes 3891204 | tf_op jit(solution)/shard_map/while/body/eval_jaxpr/qhd,khd->hqk/dot_general | solution.py:29
  73.2 1.9 %constant_dynamic-slice_fusion.10 = (bf16[128,8,128]{2,1,0:T(8,128)(2,1)}, bf16[128,8,128]{2,1,0:T(8,128)(2,1)}) fusion(bf16[192,8,128]{2,1,0:T(8,128)(2,1)} %get-tuple-element.618, s32[]{:T(128)S(6)} %select_n.189, bf16[192,8,128]{2,1,0:T(8,128)(2,1)} %get-tuple-element.615), kind=kLoop, calls=%fused_computation.29.clone.1 | loop fusion | bytes 1048580 | tf_op jit(solution)/shard_map/while/body/eval_jaxpr/dynamic_slice | solution.py:74
  75.2 1.5 %fusion.88 = (f32[8,256]{1,0:T(8,128)S(1)}, f32[8,256,128]{1,2,0:T(8,128)S(1)}) fusion(bf16[128,8,128]{2,1,0:T(8,128)(2,1)} %get-tuple-element.538, bf16[256,8,128]{2,1,0:T(8,128)(2,1)S(1)} %constant_dynamic-slice_fusion.11, pred[256,128]{0,1:T(8,128)(4,1)S(1)} %compare_and_fusion.6), kind=kOutput, calls=%fused_computation.143.clone.1 | convolution fusion | flops 68155392 | bytes 1875968 | tf_op jit(solution)/shard_map/while/body/eval_jaxpr/qhd,khd->hqk/dot_general | solution.py:29
  76.7 1.3 %bitcast_dynamic-update-slice_fusion.4 = (f32[2,8,256]{2,1,0:T(8,128)}, f32[8,256]{1,0:T(8,128)S(1)}) fusion(f32[2,8,256]{2,1,0:T(8,128)} %get-tuple-element.583, s32[]{:T(128)} %get-tuple-element.582, f32[8,256]{1,0:T(8,128)S(1)} %get-tuple-element.543, f32[8,256]{1,0:T(8,128)S(1)} %get-tuple-element.546, f32[8,256]{1,0:T(8,128)} %get-tuple-element.550), kind=kLoop, calls=%fused_computation.27.clone.1 | loop fusion | flops 4096 | bytes 41472 | tf_op jit(solution)/shard_map/while/body/jit(dynamic_update_index_in_dim)/dynamic_update_slice | solution.py:110
  78.2 2.2 %fusion.94 = f32[2,8,256,128]{3,2,1,0:T(8,128)} fusion(f32[2,8,256,128]{3,2,1,0:T(8,128)} %get-tuple-element.585, s32[]{:T(128)} %get-tuple-element.582, f32[8,256,128]{1,2,0:T(8,128)S(1)} %get-tuple-element.552, f32[8,256,192]{1,2,0:T(8,128)S(1)} %copy-done, f32[8,256,320]{1,2,0:T(8,128)S(1)} %get-tuple-element.554, ...), kind=kOutput, calls=%fused_computation.8.clone.1 | convolution fusion | flops 344719360 | bytes 7610880 | tf_op jit(solution)/shard_map/while/body/eval_jaxpr/hqk,khd->hqd/dot_general | solution.py:102
  85.5 2.2 %fusion.92 = (f32[8,256]{1,0:T(8,128)}, f32[8,256,192]{1,2,0:T(8,128)}) fusion(bf16[192,8,128]{2,1,0:T(8,128)(2,1)S(1)} %get-tuple-element.547, bf16[256,8,128]{2,1,0:T(8,128)(2,1)S(1)} %constant_dynamic-slice_fusion.11, pred[256,192]{0,1:T(8,128)(4,1)S(1)} %compare_and_fusion.8), kind=kOutput, calls=%fused_computation.145.clone.1 | convolution fusion | flops 102234112 | bytes 2547712 | tf_op jit(solution)/shard_map/while/body/eval_jaxpr/qhd,khd->hqk/dot_general | solution.py:29
  88.5 1.7 %fusion.89 = (f32[8,256]{1,0:T(8,128)S(1)}, f32[8,256,320]{1,2,0:T(8,128)S(1)}) fusion(bf16[576,8,128]{2,0,1:T(8,128)(2,1)} %get-tuple-element.613, s32[]{:T(128)S(6)} %select_n.192, bf16[256,8,128]{2,1,0:T(8,128)(2,1)S(1)} %constant_dynamic-slice_fusion.11, pred[256,320]{0,1:T(8,128)(4,1)} %compare_and_fusion.7), kind=kOutput, calls=%fused_computation.144.clone.1 | convolution fusion | flops 169736192 | bytes 3891204 | tf_op jit(solution)/shard_map/while/body/eval_jaxpr/qhd,khd->hqk/dot_general | solution.py:29
  90.2 1.9 %constant_dynamic-slice_fusion.10 = (bf16[128,8,128]{2,1,0:T(8,128)(2,1)}, bf16[128,8,128]{2,1,0:T(8,128)(2,1)}) fusion(bf16[192,8,128]{2,1,0:T(8,128)(2,1)} %get-tuple-element.618, s32[]{:T(128)S(6)} %select_n.189, bf16[192,8,128]{2,1,0:T(8,128)(2,1)} %get-tuple-element.615), kind=kLoop, calls=%fused_computation.29.clone.1 | loop fusion | bytes 1048580 | tf_op jit(solution)/shard_map/while/body/eval_jaxpr/dynamic_slice | solution.py:74
  92.2 1.5 %fusion.88 = (f32[8,256]{1,0:T(8,128)S(1)}, f32[8,256,128]{1,2,0:T(8,128)S(1)}) fusion(bf16[128,8,128]{2,1,0:T(8,128)(2,1)} %get-tuple-element.538, bf16[256,8,128]{2,1,0:T(8,128)(2,1)S(1)} %constant_dynamic-slice_fusion.11, pred[256,128]{0,1:T(8,128)(4,1)S(1)} %compare_and_fusion.6), kind=kOutput, calls=%fused_computation.143.clone.1 | convolution fusion | flops 68155392 | bytes 1875968 | tf_op jit(solution)/shard_map/while/body/eval_jaxpr/qhd,khd->hqk/dot_general | solution.py:29
  93.7 1.3 %bitcast_dynamic-update-slice_fusion.4 = (f32[2,8,256]{2,1,0:T(8,128)}, f32[8,256]{1,0:T(8,128)S(1)}) fusion(f32[2,8,256]{2,1,0:T(8,128)} %get-tuple-element.583, s32[]{:T(128)} %get-tuple-element.582, f32[8,256]{1,0:T(8,128)S(1)} %get-tuple-element.543, f32[8,256]{1,0:T(8,128)S(1)} %get-tuple-element.546, f32[8,256]{1,0:T(8,128)} %get-tuple-element.550), kind=kLoop, calls=%fused_computation.27.clone.1 | loop fusion | flops 4096 | bytes 41472 | tf_op jit(solution)/shard_map/while/body/jit(dynamic_update_index_in_dim)/dynamic_update_slice | solution.py:110
  95.2 2.2 %fusion.94 = f32[2,8,256,128]{3,2,1,0:T(8,128)} fusion(f32[2,8,256,128]{3,2,1,0:T(8,128)} %get-tuple-element.585, s32[]{:T(128)} %get-tuple-element.582, f32[8,256,128]{1,2,0:T(8,128)S(1)} %get-tuple-element.552, f32[8,256,192]{1,2,0:T(8,128)S(1)} %copy-done, f32[8,256,320]{1,2,0:T(8,128)S(1)} %get-tuple-element.554, ...), kind=kOutput, calls=%fused_computation.8.clone.1 | convolution fusion | flops 344719360 | bytes 7610880 | tf_op jit(solution)/shard_map/while/body/eval_jaxpr/hqk,khd->hqd/dot_general | solution.py:102
  98.8 1.8 %copy.52 = f32[8,2,256,128]{3,2,1,0:T(8,128)S(1)} copy(f32[8,2,256,128]{3,2,0,1:T(8,128)} %bitcast.63) | data formatting | bytes 4194304 | tf_op jit(solution)/shard_map/transpose | solution.py:113
  100.6 10.1 %conditional.2 = ((f32[8,512]{1,0:T(8,128)S(1)}, f32[8,512]{1,0:T(8,128)S(1)}, f32[8,512,128]{2,1,0:T(8,128)S(1)})) conditional(s32[]{:T(128)} %bitcast.6, (f32[8,512]{1,0:T(8,128)S(1)}, f32[8,512]{1,0:T(8,128)S(1)}, f32[8,512,128]{2,1,0:T(8,128)S(1)}) %tuple.115, (s32[512]{0:T(512)S(1)}, s32[512]{0:T(512)S(1)}, bf16[512,8,128]{2,1,0:T(8,128)(2,1)}, ...), branch_computations={%region_16.17_spmd, %region_17.20_spmd} | conditional | flops 1104421888 | bytes 38019132 | solution.py:140
  101.1 3.7 %fusion.34 = (f32[8,512]{1,0:T(8,128)S(1)}, f32[8,512,512]{1,2,0:T(8,128)S(1)}) fusion(pred[512,512]{0,1:T(8,128)(4,1)S(1)} %broadcast_compare_fusion.1, bf16[512,8,128]{2,1,0:T(8,128)(2,1)} %get-tuple-element.372, bf16[512,8,128]{2,1,0:T(8,128)(2,1)} %get-tuple-element.371), kind=kOutput, calls=%fused_computation.68 | convolution fusion | flops 545255424 | bytes 10764288 | tf_op jit(solution)/shard_map/cond/branch_1_fun/cond/branch_1_fun/qhd,khd->hqk/dot_general | solution.py:29
  104.8 2.1 %fusion.33 = f32[8,512]{1,0:T(8,128)S(1)} fusion(f32[8,512,512]{1,2,0:T(8,128)S(1)} %get-tuple-element.436, f32[8,512]{1,0:T(8,128)S(1)} %max.5, pred[512,512]{0,1:T(8,128)(4,1)S(1)} %broadcast_compare_fusion.1), kind=kLoop, calls=%fused_computation.67 | loop fusion | flops 10481664 | bytes 8683520 | tf_op jit(solution)/shard_map/cond/branch_1_fun/cond/branch_1_fun/reduce_sum | solution.py:130
  106.9 3.8 %multiply_add_fusion = f32[8,512,128]{2,1,0:T(8,128)S(1)} fusion(f32[8,512,128]{2,1,0:T(8,128)S(1)} %get-tuple-element.281, f32[8,512,512]{1,2,0:T(8,128)S(1)} %get-tuple-element.436, f32[8,512]{1,0:T(8,128)S(1)} %max.5, pred[512,512]{0,1:T(8,128)(4,1)S(1)} %broadcast_compare_fusion.1, bf16[512,8,128]{2,1,0:T(8,128)(2,1)S(1)} %copy-done.16, ...), kind=kOutput, calls=%fused_computation.71 | convolution fusion | flops 548405248 | bytes 13926400 | tf_op jit(solution)/shard_map/cond/branch_1_fun/cond/branch_1_fun/hqk,khd->hqd/dot_general | solution.py:131
  110.8 2.6 %conditional.3 = (f32[8,512]{1,0:T(8,128)S(1)}, f32[8,512,128]{2,0,1:T(8,128)}) conditional(s32[]{:T(128)} %bitcast.5, (f32[8,512]{1,0:T(8,128)S(1)}, f32[8,512,128]{2,1,0:T(8,128)S(1)}) %tuple.43, (s32[512]{0:T(512)S(1)}, bf16[512,8,128]{2,1,0:T(8,128)(2,1)}, f32[8,512]{1,0:T(8,128)S(1)}, f32[8,512]{1,0:T(8,128)S(1)}, ...), branch_computations={%region_20.21_spmd, %region_21.24_spmd} | conditional | flops 1104159232 | bytes 34836496 | solution.py:140
  110.8 2.6 %copy.62 = f32[8,512,128]{2,0,1:T(8,128)} copy(f32[8,512,128]{2,1,0:T(8,128)S(1)} %get-tuple-element.383) | data formatting | bytes 4194304 | tf_op jit(solution)/shard_map/cond | solution.py:140
  113.5 2.7 %fusion.64 = bf16[512,8,128]{2,1,0:T(8,128)(2,1)} fusion(f32[8,512,128]{2,0,1:T(8,128)} %get-tuple-element.384, f32[8,512]{0,1:T(8,128)S(1)} %copy.57), kind=kLoop, calls=%fused_computation.117 | loop fusion | flops 1048576 | bytes 3162112 | tf_op jit(solution)/shard_map/convert_element_type | solution.py:222
  (140 shorter events, 29.4 us)
Async XLA Ops:
  6.5 8.1 %copy-start.4 = (bf16[512,8,128]{2,1,0:T(8,128)(2,1)S(1)}, bf16[512,8,128]{2,1,0:T(8,128)(2,1)}, u32[]{:S(2)}) copy-start(bf16[512,8,128]{2,1,0:T(8,128)(2,1)} %param.11) | copy-start | bytes 3145732
  6.5 94.0 %all-gather.3.cloned.1.call-start = ((), (), s32[]{:S(2)}) async-start(), calls=%async_computation | async-start | bytes 1179648 | tf_op jit(solution)/shard_map/all_gather | solution.py:211
  8.8 91.8 %all-gather.5.cloned.1.call-start = ((), (), s32[]{:S(2)}) async-start(), calls=%async_computation.1 | async-start | bytes 1179648 | tf_op jit(solution)/shard_map/all_gather | solution.py:212
  10.2 9.1 %copy-start.5 = (bf16[512,8,128]{2,0,1:T(8,128)(2,1)}, bf16[512,8,128]{2,0,1:T(8,128)(2,1)S(1)}, u32[]{:S(2)}) copy-start(bf16[512,8,128]{2,0,1:T(8,128)(2,1)S(1)} %copy.39) | copy-start | bytes 3145732
  11.1 8.9 %copy-start.3 = (bf16[512,8,128]{2,1,0:T(8,128)(2,1)S(1)}, bf16[512,8,128]{2,1,0:T(8,128)(2,1)}, u32[]{:S(2)}) copy-start(bf16[512,8,128]{2,1,0:T(8,128)(2,1)} %param.10) | copy-start | bytes 3145732
  11.1 22.2 %collective-permute-start = (bf16[256,8,128]{2,0,1:T(8,128)(2,1)}, bf16[256,8,128]{2,0,1:T(8,128)(2,1)}, u32[]{:S(2)}, u32[]{:S(2)}) collective-permute-start(bf16[256,8,128]{2,0,1:T(8,128)(2,1)} %slice.36), channel_id=1, source_target_pairs={{0,2},{2,4},{4,6},{6,8},{8,10},{10,12},{12,14},{1,3},{3,5},{5,7},{... | collective-permute-start | bytes 1572872 | tf_op jit(solution)/shard_map/ppermute | solution.py:19
  15.7 36.1 %collective-permute-start.1 = (bf16[256,8,128]{2,0,1:T(8,128)(2,1)}, bf16[256,8,128]{2,0,1:T(8,128)(2,1)}, u32[]{:S(2)}, u32[]{:S(2)}) collective-permute-start(bf16[256,8,128]{2,0,1:T(8,128)(2,1)} %slice.39), channel_id=1, source_target_pairs={{0,2},{2,4},{4,6},{6,8},{8,10},{10,12},{12,14},{1,3},{3,5},{5,7},{... | collective-permute-start | bytes 1572872 | tf_op jit(solution)/shard_map/ppermute | solution.py:19
  23.5 4.1 %copy-start.8 = (f32[128,8,128]{2,1,0:T(8,128)S(1)}, f32[128,8,128]{2,1,0:T(8,128)}, u32[]{:S(2)}) copy-start(f32[128,8,128]{2,1,0:T(8,128)} %bitcast_reduce_fusion.3) | copy-start | bytes 1572868
  25.6 8.7 %copy-start.6 = (bf16[512,8,128]{2,0,1:T(8,128)(2,1)S(1)}, bf16[512,8,128]{2,0,1:T(8,128)(2,1)}, u32[]{:S(2)}) copy-start(bf16[512,8,128]{2,0,1:T(8,128)(2,1)} %copy-done.5) | copy-start | bytes 3145732
  27.6 1.9 %copy-start.14 = (s32[512]{0:T(512)}, s32[512]{0:T(512)S(1)}, u32[]{:S(2)}) copy-start(s32[512]{0:T(512)S(1)} %fusion.67) | copy-start | bytes 6148
  55.5 5.7 %copy-start.7 = (bf16[256,8,128]{2,1,0:T(8,128)(2,1)S(1)}, bf16[256,8,128]{2,1,0:T(8,128)(2,1)}, u32[]{:S(2)}) copy-start(bf16[256,8,128]{2,1,0:T(8,128)(2,1)} %multiply_convert_fusion.1) | copy-start | bytes 1572868
  57.4 5.6 %copy-start.9 = (bf16[128,8,128]{2,1,0:T(8,128)(2,1)S(1)}, bf16[128,8,128]{2,1,0:T(8,128)(2,1)}, u32[]{:S(2)}) copy-start(bf16[128,8,128]{2,1,0:T(8,128)(2,1)} %multiply_convert_fusion.3) | copy-start | bytes 786436
  64.7 1.3 %copy-start.17 = (s32[2]{0:T(128)}, s32[2]{0:T(128)S(1)}, u32[]{:S(2)}) copy-start(s32[2]{0:T(128)S(1)} %get-tuple-element.610) | copy-start | bytes 28 | tf_op jit(solution)/shard_map/while
  75.0 3.0 %copy-start.1 = (bf16[128,8,128]{2,1,0:T(8,128)(2,1)S(1)}, bf16[128,8,128]{2,1,0:T(8,128)(2,1)}, u32[]{:S(2)}) copy-start(bf16[128,8,128]{2,1,0:T(8,128)(2,1)} %get-tuple-element.556) | copy-start | bytes 786436 | tf_op jit(solution)/shard_map/while
  75.0 3.1 %copy-start.2 = (bf16[576,8,128]{2,0,1:T(8,128)(2,1)S(1)}, bf16[576,8,128]{2,0,1:T(8,128)(2,1)}, u32[]{:S(2)}) copy-start(bf16[576,8,128]{2,0,1:T(8,128)(2,1)} %get-tuple-element.616) | copy-start | bytes 3538948 | tf_op jit(solution)/shard_map/while
  75.0 3.1 %copy-start = (f32[8,256,192]{1,2,0:T(8,128)S(1)}, f32[8,256,192]{1,2,0:T(8,128)}, u32[]{:S(2)}) copy-start(f32[8,256,192]{1,2,0:T(8,128)} %get-tuple-element.553) | copy-start | bytes 4718596 | tf_op jit(solution)/shard_map/while
  80.4 0.7 copy-start.11
  80.4 1.4 %copy-start.18 = (s32[2]{0:T(128)S(1)}, s32[2]{0:T(128)}, u32[]{:S(2)}) copy-start(s32[2]{0:T(128)} %copy-done.17) | copy-start | bytes 28 | tf_op jit(solution)/shard_map/while
  81.1 0.6 copy-start.12
  81.7 1.3 %copy-start.17 = (s32[2]{0:T(128)}, s32[2]{0:T(128)S(1)}, u32[]{:S(2)}) copy-start(s32[2]{0:T(128)S(1)} %get-tuple-element.610) | copy-start | bytes 28 | tf_op jit(solution)/shard_map/while
  92.1 3.0 %copy-start.1 = (bf16[128,8,128]{2,1,0:T(8,128)(2,1)S(1)}, bf16[128,8,128]{2,1,0:T(8,128)(2,1)}, u32[]{:S(2)}) copy-start(bf16[128,8,128]{2,1,0:T(8,128)(2,1)} %get-tuple-element.556) | copy-start | bytes 786436 | tf_op jit(solution)/shard_map/while
  92.1 3.0 %copy-start.2 = (bf16[576,8,128]{2,0,1:T(8,128)(2,1)S(1)}, bf16[576,8,128]{2,0,1:T(8,128)(2,1)}, u32[]{:S(2)}) copy-start(bf16[576,8,128]{2,0,1:T(8,128)(2,1)} %get-tuple-element.616) | copy-start | bytes 3538948 | tf_op jit(solution)/shard_map/while
  92.1 3.1 %copy-start = (f32[8,256,192]{1,2,0:T(8,128)S(1)}, f32[8,256,192]{1,2,0:T(8,128)}, u32[]{:S(2)}) copy-start(f32[8,256,192]{1,2,0:T(8,128)} %get-tuple-element.553) | copy-start | bytes 4718596 | tf_op jit(solution)/shard_map/while
  97.4 0.7 copy-start.11
  97.4 1.4 %copy-start.18 = (s32[2]{0:T(128)S(1)}, s32[2]{0:T(128)}, u32[]{:S(2)}) copy-start(s32[2]{0:T(128)} %copy-done.17) | copy-start | bytes 28 | tf_op jit(solution)/shard_map/while
  98.2 0.6 copy-start.12
  98.8 1.8 %copy-start.10 = (f32[2,8,256]{2,1,0:T(8,128)S(1)}, f32[2,8,256]{2,1,0:T(8,128)}, u32[]{:S(2)}) copy-start(f32[2,8,256]{2,1,0:T(8,128)} %get-tuple-element.296) | copy-start | bytes 49156
  98.8 1.9 %copy-start.13 = (f32[2,8,256]{2,1,0:T(8,128)S(1)}, f32[2,8,256]{2,1,0:T(8,128)}, u32[]{:S(2)}) copy-start(f32[2,8,256]{2,1,0:T(8,128)} %get-tuple-element.297) | copy-start | bytes 49156
  98.8 1.9 %copy-start.15 = (s32[512]{0:T(512)S(1)}, s32[512]{0:T(512)}, u32[]{:S(2)}) copy-start(s32[512]{0:T(512)} %copy-done.14) | copy-start | bytes 6148
  104.8 2.1 %copy-start.16 = (bf16[512,8,128]{2,1,0:T(8,128)(2,1)S(1)}, bf16[512,8,128]{2,1,0:T(8,128)(2,1)}, u32[]{:S(2)}) copy-start(bf16[512,8,128]{2,1,0:T(8,128)(2,1)} %get-tuple-element.376) | copy-start | bytes 3145732 | tf_op jit(solution)/shard_map/cond/branch_1_fun/cond
Sparse Core Ops, SparseCore 0:
  9.5 44.1 all-gather.2
  55.7 38.2 all-gather.4
where the time goes:
time: 124 us; the launch traced here: 123 us
  other arithmetic  33 us (27%)
  local copies, waits for them, and re-layouts  23.5 us (19%)
  matrix products  22.6 us (18%)
  waiting for transfers between devices  19.9 us (16%)
  between operations  15 us (12%)
  starting transfers between devices  7.01 us (6%)
  loops' own time  2.05 us (2%)
    ppermute x2, waiting for transfers between devices, passed_along(): lax.ppermute(value, axis, [(source, source + steps) for source in range(i...  19.8 us
    dot_general x7, matrix products, level_scores(): jnp.einsum('qhd,khd->hqk', query_block, key_rows, preferred_element_type=...  14.4 us
    reduce_sum x10, other arithmetic, pool_rows(): return jnp.mean(grouped, axis=1).astype(jnp.bfloat16)  10.3 us
    ppermute x2, starting transfers between devices, passed_along(): lax.ppermute(value, axis, [(source, source + steps) for source in range(i...  6.97 us
    convert_element_type x10, other arithmetic, pool_rows(): return jnp.mean(grouped, axis=1).astype(jnp.bfloat16)  5.59 us
    dot_general x2, matrix products, one_block(): jnp.einsum('hqk,khd->hqd', weights.astype(jnp.bfloat16), value_rows, pref...  4.4 us
    dot_general x1, matrix products, work(): jnp.einsum('hqk,khd->hqd', weights.astype(jnp.bfloat16), block_v, preferr...  3.8 us
    dynamic_slice x4, local copies, waits for them, and re-layouts, one_block(): val2 = lax.dynamic_slice_in_dim(ext2_v, local // 4, quad // 4 + BLOCK, 0)  3.79 us
  transfers between devices with their start and end apart: 4, of which 2 were waited for; matrix products, arithmetic and copies ran while one was open for 49% of the time, Pallas kernels for 0%

commit v1 on v0

v1 whole, which is shorter than its diff:
```python
import functools
import math

import jax
import jax.numpy as jnp
from jax import lax
from jax.experimental import pallas as pl
from jax.experimental.pallas import tpu as pltpu
from jax.sharding import PartitionSpec as P

BLOCK = 64
QUAD = 4 * BLOCK
PAIR = 2 * BLOCK
NEG = -1e30
F32 = jnp.float32
BF16 = jnp.bfloat16
VMEM = pl.BlockSpec(memory_space=pltpu.VMEM)
SMEM = pl.BlockSpec(memory_space=pltpu.SMEM)


def shifted(value, axis, steps):
    count = lax.axis_size(axis)
    return lax.ppermute(value, axis, [(i, i + steps) for i in range(count - steps)])


def pooled(block, factor):
    count = block.shape[0] // factor
    grouped = block.reshape(count, factor, block.shape[1], block.shape[2])
    total = grouped[:, 0]
    for i in range(1, factor):
        total = total + grouped[:, i]
    return total * (1.0 / factor)


def flat(block):
    return block.reshape(block.shape[0] * block.shape[1], block.shape[2])


def prep_kernel(k_ref, v_ref, halo_ref, far_ref, tok):
    rows, heads, width = k_ref.shape
    for side, ref in enumerate((k_ref, v_ref)):
        base = 0
        for chunk in range(rows // BLOCK):
            block = ref[pl.ds(chunk * BLOCK, BLOCK)].astype(F32)
            part = flat(pooled(block, 8))
            tok[pl.ds(base, part.shape[0])] = part
            base += part.shape[0]
        near = ref[pl.ds(rows - BLOCK, BLOCK)].astype(F32)
        tok[pl.ds(base, BLOCK * heads)] = flat(near)
        level1 = pooled(ref[pl.ds(rows - 2 * BLOCK, BLOCK)].astype(F32), 2)
        tok[pl.ds(base + BLOCK * heads, BLOCK * heads // 2)] = flat(level1)
        level2 = pooled(ref[pl.ds(rows - QUAD, 2 * BLOCK)].astype(F32), 4)
        tok[pl.ds(base + BLOCK * heads * 3 // 2, BLOCK * heads // 2)] = flat(level2)
        for head in range(heads):
            far_ref[side, head] = tok[pl.ds(head, rows // 8, stride=heads)].astype(BF16)
            halo_ref[side, head] = tok[pl.ds(base + head, 2 * BLOCK, stride=heads)].astype(BF16)


def prep(keys, values):
    rows, heads, width = keys.shape
    return pl.pallas_call(
        prep_kernel,
        out_shape=(
            jax.ShapeDtypeStruct((2, heads, 2 * BLOCK, width), BF16),
            jax.ShapeDtypeStruct((2, heads, rows // 8, width), BF16),
        ),
        in_specs=[VMEM, VMEM],
        out_specs=(VMEM, VMEM),
        scratch_shapes=[pltpu.VMEM(((rows // 8 + 2 * BLOCK) * heads, width), F32)],
        name="prep",
    )(keys, values)


def local_kernel(me_ref, q_ref, k_ref, v_ref, halo_ref, qh_ref, acc_ref, stat_ref, tok, tmp, bias, *ext):
    rows, heads, width = k_ref.shape
    scale = math.log2(math.e) / math.sqrt(width)
    pairs = rows // PAIR
    first = me_ref[0] == 0
    columns = 5 * BLOCK

    def spread(ref, factor, target, lead):
        for chunk in range(rows // BLOCK):
            block = ref[pl.ds(chunk * BLOCK, BLOCK)].astype(F32)
            part = flat(block if factor == 1 else pooled(block, factor))
            tok[pl.ds(chunk * part.shape[0], part.shape[0])] = part
        for head in range(heads):
            target[head, pl.ds(lead, rows // factor)] = tok[pl.ds(head, rows // factor, stride=heads)].astype(BF16)

    spread(q_ref, 1, qh_ref, 0)
    for side, ref in enumerate((k_ref, v_ref)):
        ext0, ext1, ext2 = ext[3 * side : 3 * side + 3]
        spread(ref, 1, ext0, BLOCK)
        spread(ref, 2, ext1, BLOCK)
        spread(ref, 4, ext2, BLOCK)
        for head in range(heads):
            near = halo_ref[side, head, :BLOCK]
            level1 = halo_ref[side, head, BLOCK : BLOCK * 3 // 2]
            tmp[:BLOCK] = near.astype(F32)
            tmp[BLOCK : BLOCK * 3 // 2] = level1.astype(F32)
            ext0[head, :BLOCK] = near
            ext1[head, : BLOCK // 2] = level1
            ext1[head, BLOCK // 2 : BLOCK] = (
                (tmp[pl.ds(0, BLOCK // 2, stride=2)] + tmp[pl.ds(1, BLOCK // 2, stride=2)]) * 0.5
            ).astype(BF16)
            ext2[head, : BLOCK // 2] = halo_ref[side, head, BLOCK * 3 // 2 :]
            ext2[head, BLOCK // 2 : BLOCK * 3 // 4] = (
                (tmp[pl.ds(BLOCK, BLOCK // 4, stride=2)] + tmp[pl.ds(BLOCK + 1, BLOCK // 4, stride=2)]) * 0.5
            ).astype(BF16)
            ext2[head, BLOCK * 3 // 4 : BLOCK] = (
                (
                    (tmp[pl.ds(0, BLOCK // 4, stride=4)] + tmp[pl.ds(1, BLOCK // 4, stride=4)])
                    + (tmp[pl.ds(2, BLOCK // 4, stride=4)] + tmp[pl.ds(3, BLOCK // 4, stride=4)])
                )
                * 0.25
            ).astype(BF16)

    row = lax.broadcasted_iota(jnp.int32, (PAIR, columns), 0)
    col = lax.broadcasted_iota(jnp.int32, (PAIR, columns), 1)
    late = row >= BLOCK
    is0 = col < 3 * BLOCK
    is1 = (col >= 3 * BLOCK) & (col < 4 * BLOCK)
    is2 = col >= 4 * BLOCK
    ok0 = is0 & (col - BLOCK <= row) & ((col >= BLOCK) | ~late)
    ok1 = is1 & ((col < 3 * BLOCK + BLOCK // 2) | late)
    for pair in range(4):
        ok2 = is2 & (col < 4 * BLOCK + BLOCK // 2) if pair % 2 == 0 else is2
        ok = ok0 | ok1 | ok2
        if pair == 0:
            ok = ok & ((is0 & (col >= BLOCK)) | ~first)
        if pair == 1:
            ok = ok & (~is2 | ~first)
        level = jnp.where(is0, 0.0, jnp.where(is1, 1.0, 2.0))
        bias[pair] = jnp.where(ok, level, NEG)

    lane = lax.broadcasted_iota(jnp.int32, (PAIR, width), 1)
    for pair in range(pairs):
        kind = pair if pair < 2 else 2 + pair % 2
        base2 = pair // 2 * BLOCK

        def one_head(head, stats):
            def rows_of(side):
                ext0, ext1, ext2 = ext[3 * side : 3 * side + 3]
                return jnp.concatenate(
                    [
                        ext0[head, pl.ds(PAIR * pair, 3 * BLOCK)],
                        ext1[head, pl.ds(BLOCK * pair, BLOCK)],
                        ext2[head, pl.ds(base2, BLOCK)],
                    ],
                    0,
                )

            query = qh_ref[head, pl.ds(PAIR * pair, PAIR)]
            score = lax.dot_general(query, rows_of(0), (((1,), (1,)), ((), ())), preferred_element_type=F32)
            score = score * scale + bias[kind]
            top = jnp.max(score, axis=1, keepdims=True)
            weight = jnp.exp2(score - top)
            total = jnp.sum(weight, axis=1, keepdims=True)
            acc_ref[head, pl.ds(PAIR * pair, PAIR)] = jnp.dot(
                weight.astype(BF16), rows_of(1), preferred_element_type=F32
            )
            stats = jnp.where(lane == head, top, stats)
            return jnp.where(lane == head + heads, total, stats)

        stats = jnp.zeros((PAIR, width), F32)
        for head in range(heads):
            stats = one_head(head, stats)
        stat_ref[pl.ds(PAIR * pair, PAIR)] = stats


def local(me, queries, keys, values, halo):
    rows, heads, width = keys.shape
    side = [
        pltpu.VMEM((heads, BLOCK + rows // factor, width), BF16) for factor in (1, 2, 4)
    ]
    return pl.pallas_call(
        local_kernel,
        out_shape=(
            jax.ShapeDtypeStruct((heads, rows, width), BF16),
            jax.ShapeDtypeStruct((heads, rows, width), F32),
            jax.ShapeDtypeStruct((rows, width), F32),
        ),
        in_specs=[SMEM, VMEM, VMEM, VMEM, VMEM],
        out_specs=(VMEM, VMEM, VMEM),
        scratch_shapes=[
            pltpu.VMEM((rows * heads, width), F32),
            pltpu.VMEM((BLOCK * 3 // 2, width), F32),
            pltpu.VMEM((4, PAIR, 5 * BLOCK), F32),
        ]
        + side
        + side,
        name="local",
    )(me, queries, keys, values, halo)


def far_kernel(sources, me_ref, qh_ref, acc_ref, stat_ref, *refs):
    chunks, (out_ref, tok) = refs[:-2], refs[-2:]
    heads, tile, width = qh_ref.shape
    count = chunks[0].shape[-2]
    scale = math.log2(math.e) / math.sqrt(width)
    me = me_ref[0]
    quad = pl.program_id(0) * tile // QUAD
    limit = me * count + (quad - 1) * (QUAD // 8)
    columns = count * len(chunks)
    col = lax.broadcasted_iota(jnp.int32, (1, columns), 1)
    bias = jnp.full((1, columns), NEG, F32)
    for at, back in enumerate(sources):
        ours = (col >= at * count) & (col < (at + 1) * count)
        number = (me - back) * count + col - at * count
        ours = ours & (number < limit) & (me >= back)
        bias = jnp.where(ours, 3.0, bias)
    for head in range(heads):
        kept = jnp.concatenate([chunk[0, head] for chunk in chunks], 0)
        score = lax.dot_general(qh_ref[head], kept, (((1,), (1,)), ((), ())), preferred_element_type=F32)
        score = score * scale + bias
        before = stat_ref[:, head : head + 1]
        top = jnp.maximum(before, jnp.max(score, axis=1, keepdims=True))
        fade = jnp.exp2(before - top)
        weight = jnp.exp2(score - top)
        total = stat_ref[:, heads + head : heads + head + 1] * fade + jnp.sum(weight, axis=1, keepdims=True)
        kept = jnp.concatenate([chunk[1, head] for chunk in chunks], 0)
        summed = acc_ref[head] * fade + jnp.dot(weight.astype(BF16), kept, preferred_element_type=F32)
        tok[pl.ds(head, tile, stride=heads)] = summed * (1.0 / total)
    out_ref[...] = tok[...].reshape(tile, heads, width).astype(BF16)


def far(me, qh, acc, stat, chunks, sources):
    heads, rows, width = qh.shape
    tile = PAIR
    return pl.pallas_call(
        functools.partial(far_kernel, sources),
        out_shape=jax.ShapeDtypeStruct((rows, heads, width), BF16),
        grid=(rows // tile,),
        in_specs=[
            SMEM,
            pl.BlockSpec((heads, tile, width), lambda i: (0, i, 0)),
            pl.BlockSpec((heads, tile, width), lambda i: (0, i, 0)),
            pl.BlockSpec((tile, width), lambda i: (i, 0)),
        ]
        + [VMEM] * len(chunks),
        out_specs=pl.BlockSpec((tile, heads, width), lambda i: (i, 0, 0)),
        scratch_shapes=[pltpu.VMEM((tile * heads, width), F32)],
        name="far",
    )(me, qh, acc, stat, *chunks)


def shards(queries, keys, values):
    count = lax.axis_size("seq")
    me = lax.axis_index("seq").reshape(1)
    halo, own = prep(keys, values)
    halo = shifted(halo, "seq", 1)
    sources = tuple(range(1, count))
    chunks = [shifted(own, "seq", back) for back in sources]
    qh, acc, stat = local(me, queries, keys, values, halo)
    return far(me, qh, acc, stat, chunks, sources)


def solution(mesh):
    spec = P(("groups", "seq"), "heads", None)
    return jax.shard_map(
        shards,
        mesh=mesh,
        in_specs=(spec, spec, spec),
        out_specs=spec,
        check_vma=False,
    )
```

time: 124 us -> 82 us (0.66)
  Pallas kernels: 0 us -> 33 us
  other arithmetic: 33 us -> 0 us
  local copies, waits for them, and re-layouts: 23.5 us -> 0.69 us
  matrix products: 22.6 us -> 0 us
  starting transfers between devices: 7.01 us -> 26.3 us
  between operations: 15 us -> 0.18 us
  loops' own time: 2.05 us -> 0 us
  waiting for transfers between devices: 19.9 us -> 21.6 us
    pallas_call x0 -> x3, Pallas kernels: none -> 33 us  [the longest x1 16.3 us: far(): pl.pallas_call(functools.partial(far_kernel, sources), out_shape=jax.Shap...]
    dot_general x10 -> x0, matrix products: 22.6 us -> none  [the longest x7 14.4 us: level_scores(): jnp.einsum('qhd,khd->hqk', query_block, key_rows, preferred_element_type=...]
    ppermute x2 -> x8, starting transfers between devices: 6.97 us -> 26.3 us  [shifted(): lax.ppermute(value, axis, [(i, i + steps) for i in range(count - steps)])]
    reduce_sum x13 -> x0, other arithmetic: 13.8 us -> none  [the longest x10 10.3 us: pool_rows(): return jnp.mean(grouped, axis=1).astype(jnp.bfloat16)]
    dynamic_slice x14 -> x0, local copies, waits for them, and re-layouts: 9.71 us -> none  [the longest x4 3.79 us: one_block(): val2 = lax.dynamic_slice_in_dim(ext2_v, local // 4, quad // 4 + BLOCK, 0)]
    convert_element_type x11 -> x0, other arithmetic: 8.32 us -> none  [the longest x10 5.59 us: pool_rows(): return jnp.mean(grouped, axis=1).astype(jnp.bfloat16)]
    slice x7 -> x0, local copies, waits for them, and re-layouts: 6.16 us -> none  [the longest x1 1.01 us: shards(): tail_v[quad - 2 * BLOCK:]]
    concatenate x6 -> x0, other arithmetic: 5.75 us -> none  [the longest x1 1.15 us: shards(): ext0_v = jnp.concatenate([lead[1], values], 0)]
  transfers between devices with their start and end apart: 4 -> 8, of which waited for: 2 -> 2; matrix products, arithmetic and copies ran while one was open for 49% -> 0% of each run, Pallas kernels for 0% -> 17%
where the time goes in v1:
time: 82 us; the launch traced here: 81.7 us
  Pallas kernels  33 us (40%)
  starting transfers between devices  26.3 us (32%)
  waiting for transfers between devices  21.6 us (26%)
    ppermute x8, starting transfers between devices, shifted(): lax.ppermute(value, axis, [(i, i + steps) for i in range(count - steps)])  26.3 us
    ppermute x8, waiting for transfers between devices, shifted(): lax.ppermute(value, axis, [(i, i + steps) for i in range(count - steps)])  21.6 us
    pallas_call x1, Pallas kernels, far(): pl.pallas_call(functools.partial(far_kernel, sources), out_shape=jax.Shap...  16.3 us
    pallas_call x1, Pallas kernels, local(): pl.pallas_call(local_kernel, out_shape=(jax.ShapeDtypeStruct((heads, rows...  13.6 us
    pallas_call x1, Pallas kernels, prep(): pl.pallas_call(prep_kernel, out_shape=(jax.ShapeDtypeStruct((2, heads, 2...  3.05 us
  transfers between devices with their start and end apart: 8, of which 2 were waited for; matrix products, arithmetic and copies ran while one was open for 0% of the time, Pallas kernels for 17%

profile of v1, /device:TPU:16, one launch (start us, length us, event | category | flops | bytes accessed | tf_op | source)
XLA Modules:
  0.0 81.7 jit_solution(17488373534465793943)
XLA Ops:
  0.0 3.1 %prep.1 = (bf16[2,8,128,128]{3,2,1,0:T(8,128)(2,1)}, bf16[2,8,64,128]{3,2,1,0:T(8,128)(2,1)}) custom-call(bf16[512,8,128]{2,1,0:T(8,128)(2,1)} %k_ref.3, bf16[512,8,128]{2,1,0:T(8,128)(2,1)} %v_ref.3), custom_call_target="tpu_custom_call" | custom-call | tf_op jit(solution)/shard_map/prep/pallas_call | solution.py:61
  3.1 3.4 %collective-permute-start = (bf16[2,8,128,128]{3,2,1,0:T(8,128)(2,1)}, bf16[2,8,128,128]{3,2,1,0:T(8,128)(2,1)S(1)}, u32[]{:S(2)}, u32[]{:S(2)}) collective-permute-start(bf16[2,8,128,128]{3,2,1,0:T(8,128)(2,1)} %get-tuple-element.10), channel_id=1, source_target_pairs={{0,2},{2,4},{4,6},{6,8},{8,10},{10,12},{12,14},{1,3},{3,5},{5,7},{... | collective-permute-start | bytes 1572872 | tf_op jit(solution)/shard_map/ppermute | solution.py:23
  6.5 0.7 collective-permute-start.7
  7.1 0.7 collective-permute-start.6
  7.8 0.7 collective-permute-start.5
  8.5 1.3 %collective-permute-start.4 = (bf16[2,8,64,128]{3,2,1,0:T(8,128)(2,1)}, bf16[2,8,64,128]{3,2,1,0:T(8,128)(2,1)S(1)}, u32[]{:S(2)}, u32[]{:S(2)}) collective-permute-start(bf16[2,8,64,128]{3,2,1,0:T(8,128)(2,1)} %get-tuple-element.14), channel_id=1, source_target_pairs={{0,8},{2,10},{4,12},{6,14},{1,9},{3,11},{5,13},{7,15},{16,24},{18,... | collective-permute-start | bytes 786440 | tf_op jit(solution)/shard_map/ppermute | solution.py:23
  9.8 0.0 collective-permute-done.7.refs_6_
  9.8 0.0 copy-start.1
  9.8 13.0 %collective-permute-start.3 = (bf16[2,8,64,128]{3,2,1,0:T(8,128)(2,1)}, bf16[2,8,64,128]{3,2,1,0:T(8,128)(2,1)S(1)}, u32[]{:S(2)}, u32[]{:S(2)}) collective-permute-start(bf16[2,8,64,128]{3,2,1,0:T(8,128)(2,1)} %get-tuple-element.14), channel_id=1, source_target_pairs={{0,6},{2,8},{4,10},{6,12},{8,14},{1,7},{3,9},{5,11},{7,13},{9,15},... | collective-permute-start | bytes 786440 | tf_op jit(solution)/shard_map/ppermute | solution.py:23
  22.9 0.0 collective-permute-done.6.refs_5_
  22.9 0.0 copy-start.2
  22.9 4.6 %collective-permute-start.2 = (bf16[2,8,64,128]{3,2,1,0:T(8,128)(2,1)}, bf16[2,8,64,128]{3,2,1,0:T(8,128)(2,1)S(1)}, u32[]{:S(2)}, u32[]{:S(2)}) collective-permute-start(bf16[2,8,64,128]{3,2,1,0:T(8,128)(2,1)} %get-tuple-element.14), channel_id=1, source_target_pairs={{0,4},{2,6},{4,8},{6,10},{8,12},{10,14},{1,5},{3,7},{5,9},{7,11},{... | collective-permute-start | bytes 786440 | tf_op jit(solution)/shard_map/ppermute | solution.py:23
  27.6 15.8 %collective-permute-done.halo_ref = bf16[2,8,128,128]{3,2,1,0:T(8,128)(2,1)S(1)} collective-permute-done((bf16[2,8,128,128]{3,2,1,0:T(8,128)(2,1)}, bf16[2,8,128,128]{3,2,1,0:T(8,128)(2,1)S(1)}, u32[]{:S(2)}, u32[]{:S(2)}) %collective-permute-start) | collective-permute-done | bytes 524320 | tf_op jit(solution)/shard_map/ppermute | solution.py:23
  43.3 1.9 %collective-permute-start.1 = (bf16[2,8,64,128]{3,2,1,0:T(8,128)(2,1)}, bf16[2,8,64,128]{3,2,1,0:T(8,128)(2,1)S(1)}, u32[]{:S(2)}, u32[]{:S(2)}) collective-permute-start(bf16[2,8,64,128]{3,2,1,0:T(8,128)(2,1)} %get-tuple-element.14), channel_id=1, source_target_pairs={{0,2},{2,4},{4,6},{6,8},{8,10},{10,12},{12,14},{1,3},{3,5},{5,7},{... | collective-permute-start | bytes 786440 | tf_op jit(solution)/shard_map/ppermute | solution.py:23
  45.2 0.0 copy-done
  45.2 13.6 %local.1 = (bf16[8,512,128]{2,1,0:T(8,128)(2,1)}, f32[8,512,128]{2,1,0:T(8,128)}, f32[512,128]{1,0:T(8,128)}) custom-call(s32[1]{0:T(128)} %bitcast.me_ref, bf16[512,8,128]{2,1,0:T(8,128)(2,1)} %q_ref.1, bf16[512,8,128]{2,1,0:T(8,128)(2,1)} %k_ref.3, bf16[512,8,128]{2,1,0:T(8,128)(2,1)} %v_ref.3, bf16[2,8,128,128]{3,2,1,0:T(8,128)(2,1)} %copy-done), custom_call_target="tpu_custom_call" | custom-call | tf_op jit(solution)/shard_map/local/pallas_call | solution.py:175
  58.8 0.0 collective-permute-done.5.refs_4_
  58.9 0.0 collective-permute-done.4.refs_3_
  58.9 0.0 copy-start.4
  58.9 0.0 collective-permute-done.3.refs_2_
  58.9 0.0 copy-start.5
  58.9 0.0 collective-permute-done.2.refs_1_
  58.9 0.0 copy-start.6
  58.9 5.8 %collective-permute-done.1.refs_0_ = bf16[2,8,64,128]{3,2,1,0:T(8,128)(2,1)S(1)} collective-permute-done((bf16[2,8,64,128]{3,2,1,0:T(8,128)(2,1)}, bf16[2,8,64,128]{3,2,1,0:T(8,128)(2,1)S(1)}, u32[]{:S(2)}, u32[]{:S(2)}) %collective-permute-start.1) | collective-permute-done | bytes 262176 | tf_op jit(solution)/shard_map/ppermute | solution.py:23
  64.7 0.0 copy-done.1
  64.7 0.0 copy-done.2
  64.7 0.0 copy-done.3
  64.7 0.0 copy-done.4
  64.7 0.0 copy-done.5
  64.7 0.0 copy-done.6
  64.7 0.7 copy-done.7
  65.4 16.3 %far.1 = bf16[512,8,128]{2,1,0:T(8,128)(2,1)} custom-call(s32[1]{0:T(128)} %bitcast.me_ref, bf16[8,512,128]{2,1,0:T(8,128)(2,1)} %get-tuple-element.11.qh_ref, f32[8,512,128]{2,1,0:T(8,128)} %get-tuple-element.12.acc_ref, f32[512,128]{1,0:T(8,128)} %get-tuple-element.13.stat_ref, bf16[2,8,64,128]{3,2,1,0:T(8,128)(2,1)} %copy-done.7, ...), custom_call_target="tpu_custom_call" | custom-call | tf_op jit(solution)/shard_map/far/pallas_call | solution.py:229
  (3 shorter events, 0.0 us)
Async XLA Ops:
  3.1 40.3 %collective-permute-start = (bf16[2,8,128,128]{3,2,1,0:T(8,128)(2,1)}, bf16[2,8,128,128]{3,2,1,0:T(8,128)(2,1)S(1)}, u32[]{:S(2)}, u32[]{:S(2)}) collective-permute-start(bf16[2,8,128,128]{3,2,1,0:T(8,128)(2,1)} %get-tuple-element.10), channel_id=1, source_target_pairs={{0,2},{2,4},{4,6},{6,8},{8,10},{10,12},{12,14},{1,3},{3,5},{5,7},{... | collective-permute-start | bytes 1572872 | tf_op jit(solution)/shard_map/ppermute | solution.py:23
  6.5 3.4 %collective-permute-start.7 = (bf16[2,8,64,128]{3,2,1,0:T(8,128)(2,1)}, bf16[2,8,64,128]{3,2,1,0:T(8,128)(2,1)S(1)}, u32[]{:S(2)}, u32[]{:S(2)}) collective-permute-start(bf16[2,8,64,128]{3,2,1,0:T(8,128)(2,1)} %get-tuple-element.14), channel_id=1, source_target_pairs={{0,14},{1,15},{16,30},{17,31}} | collective-permute-start | bytes 786440 | tf_op jit(solution)/shard_map/ppermute | solution.py:23
  7.1 15.7 %collective-permute-start.6 = (bf16[2,8,64,128]{3,2,1,0:T(8,128)(2,1)}, bf16[2,8,64,128]{3,2,1,0:T(8,128)(2,1)S(1)}, u32[]{:S(2)}, u32[]{:S(2)}) collective-permute-start(bf16[2,8,64,128]{3,2,1,0:T(8,128)(2,1)} %get-tuple-element.14), channel_id=1, source_target_pairs={{0,12},{2,14},{1,13},{3,15},{16,28},{18,30},{17,29},{19,31}} | collective-permute-start | bytes 786440 | tf_op jit(solution)/shard_map/ppermute | solution.py:23
  7.8 51.0 %collective-permute-start.5 = (bf16[2,8,64,128]{3,2,1,0:T(8,128)(2,1)}, bf16[2,8,64,128]{3,2,1,0:T(8,128)(2,1)S(1)}, u32[]{:S(2)}, u32[]{:S(2)}) collective-permute-start(bf16[2,8,64,128]{3,2,1,0:T(8,128)(2,1)} %get-tuple-element.14), channel_id=1, source_target_pairs={{0,10},{2,12},{4,14},{1,11},{3,13},{5,15},{16,26},{18,28},{20,30},... | collective-permute-start | bytes 786440 | tf_op jit(solution)/shard_map/ppermute | solution.py:23
  8.5 50.3 %collective-permute-start.4 = (bf16[2,8,64,128]{3,2,1,0:T(8,128)(2,1)}, bf16[2,8,64,128]{3,2,1,0:T(8,128)(2,1)S(1)}, u32[]{:S(2)}, u32[]{:S(2)}) collective-permute-start(bf16[2,8,64,128]{3,2,1,0:T(8,128)(2,1)} %get-tuple-element.14), channel_id=1, source_target_pairs={{0,8},{2,10},{4,12},{6,14},{1,9},{3,11},{5,13},{7,15},{16,24},{18,... | collective-permute-start | bytes 786440 | tf_op jit(solution)/shard_map/ppermute | solution.py:23
  9.8 54.9 %copy-start.1 = (bf16[2,8,64,128]{3,2,1,0:T(8,128)(2,1)}, bf16[2,8,64,128]{3,2,1,0:T(8,128)(2,1)S(1)}, u32[]{:S(2)}) copy-start(bf16[2,8,64,128]{3,2,1,0:T(8,128)(2,1)S(1)} %collective-permute-done.7.refs_6_) | copy-start | bytes 786436
  9.8 49.0 %collective-permute-start.3 = (bf16[2,8,64,128]{3,2,1,0:T(8,128)(2,1)}, bf16[2,8,64,128]{3,2,1,0:T(8,128)(2,1)S(1)}, u32[]{:S(2)}, u32[]{:S(2)}) collective-permute-start(bf16[2,8,64,128]{3,2,1,0:T(8,128)(2,1)} %get-tuple-element.14), channel_id=1, source_target_pairs={{0,6},{2,8},{4,10},{6,12},{8,14},{1,7},{3,9},{5,11},{7,13},{9,15},... | collective-permute-start | bytes 786440 | tf_op jit(solution)/shard_map/ppermute | solution.py:23
  22.9 41.8 %copy-start.2 = (bf16[2,8,64,128]{3,2,1,0:T(8,128)(2,1)}, bf16[2,8,64,128]{3,2,1,0:T(8,128)(2,1)S(1)}, u32[]{:S(2)}) copy-start(bf16[2,8,64,128]{3,2,1,0:T(8,128)(2,1)S(1)} %collective-permute-done.6.refs_5_) | copy-start | bytes 786436
  22.9 36.0 %collective-permute-start.2 = (bf16[2,8,64,128]{3,2,1,0:T(8,128)(2,1)}, bf16[2,8,64,128]{3,2,1,0:T(8,128)(2,1)S(1)}, u32[]{:S(2)}, u32[]{:S(2)}) collective-permute-start(bf16[2,8,64,128]{3,2,1,0:T(8,128)(2,1)} %get-tuple-element.14), channel_id=1, source_target_pairs={{0,4},{2,6},{4,8},{6,10},{8,12},{10,14},{1,5},{3,7},{5,9},{7,11},{... | collective-permute-start | bytes 786440 | tf_op jit(solution)/shard_map/ppermute | solution.py:23
  43.3 1.9 %copy-start = (bf16[2,8,128,128]{3,2,1,0:T(8,128)(2,1)}, bf16[2,8,128,128]{3,2,1,0:T(8,128)(2,1)S(1)}, u32[]{:S(2)}) copy-start(bf16[2,8,128,128]{3,2,1,0:T(8,128)(2,1)S(1)} %collective-permute-done.halo_ref) | copy-start | bytes 1572868
  43.3 21.4 %collective-permute-start.1 = (bf16[2,8,64,128]{3,2,1,0:T(8,128)(2,1)}, bf16[2,8,64,128]{3,2,1,0:T(8,128)(2,1)S(1)}, u32[]{:S(2)}, u32[]{:S(2)}) collective-permute-start(bf16[2,8,64,128]{3,2,1,0:T(8,128)(2,1)} %get-tuple-element.14), channel_id=1, source_target_pairs={{0,2},{2,4},{4,6},{6,8},{8,10},{10,12},{12,14},{1,3},{3,5},{5,7},{... | collective-permute-start | bytes 786440 | tf_op jit(solution)/shard_map/ppermute | solution.py:23
  58.8 5.9 %copy-start.3 = (bf16[2,8,64,128]{3,2,1,0:T(8,128)(2,1)}, bf16[2,8,64,128]{3,2,1,0:T(8,128)(2,1)S(1)}, u32[]{:S(2)}) copy-start(bf16[2,8,64,128]{3,2,1,0:T(8,128)(2,1)S(1)} %collective-permute-done.5.refs_4_) | copy-start | bytes 786436
  58.9 5.9 %copy-start.4 = (bf16[2,8,64,128]{3,2,1,0:T(8,128)(2,1)}, bf16[2,8,64,128]{3,2,1,0:T(8,128)(2,1)S(1)}, u32[]{:S(2)}) copy-start(bf16[2,8,64,128]{3,2,1,0:T(8,128)(2,1)S(1)} %collective-permute-done.4.refs_3_) | copy-start | bytes 786436
  58.9 5.8 %copy-start.5 = (bf16[2,8,64,128]{3,2,1,0:T(8,128)(2,1)}, bf16[2,8,64,128]{3,2,1,0:T(8,128)(2,1)S(1)}, u32[]{:S(2)}) copy-start(bf16[2,8,64,128]{3,2,1,0:T(8,128)(2,1)S(1)} %collective-permute-done.3.refs_2_) | copy-start | bytes 786436
  58.9 5.8 %copy-start.6 = (bf16[2,8,64,128]{3,2,1,0:T(8,128)(2,1)}, bf16[2,8,64,128]{3,2,1,0:T(8,128)(2,1)S(1)}, u32[]{:S(2)}) copy-start(bf16[2,8,64,128]{3,2,1,0:T(8,128)(2,1)S(1)} %collective-permute-done.2.refs_1_) | copy-start | bytes 786436
  64.7 0.7 copy-start.7

commit v2 on v1

--- a/solution.py
+++ b/solution.py
@@ -67,32 +67,35 @@
         in_specs=[VMEM, VMEM],
         out_specs=(VMEM, VMEM),
         scratch_shapes=[pltpu.VMEM(((rows // 8 + 2 * BLOCK) * heads, width), F32)],
+        compiler_params=pltpu.CompilerParams(vmem_limit_bytes=28 << 20),
         name="prep",
     )(keys, values)
 
 
-def local_kernel(me_ref, q_ref, k_ref, v_ref, halo_ref, qh_ref, acc_ref, stat_ref, tok, tmp, bias, *ext):
+def local_kernel(me_ref, q_ref, k_ref, v_ref, halo_ref, qh_ref, acc_ref, top_ref, tok, tmp, bias, *ext):
     rows, heads, width = k_ref.shape
     scale = math.log2(math.e) / math.sqrt(width)
     pairs = rows // PAIR
     first = me_ref[0] == 0
     columns = 5 * BLOCK
 
-    def spread(ref, factor, target, lead):
+    for chunk in range(rows // BLOCK):
+        tok[pl.ds(chunk * BLOCK * heads, BLOCK * heads)] = flat(q_ref[pl.ds(chunk * BLOCK, BLOCK)].astype(F32))
+    for head in range(heads):
+        qh_ref[head] = tok[pl.ds(head, rows, stride=heads)].astype(BF16)
+    for side, ref in enumerate((k_ref, v_ref)):
+        ext0, ext1, ext2 = ext[3 * side : 3 * side + 3]
         for chunk in range(rows // BLOCK):
             block = ref[pl.ds(chunk * BLOCK, BLOCK)].astype(F32)
-            part = flat(block if factor == 1 else pooled(block, factor))
-            tok[pl.ds(chunk * part.shape[0], part.shape[0])] = part
-        for head in range(heads):
-            target[head, pl.ds(lead, rows // factor)] = tok[pl.ds(head, rows // factor, stride=heads)].astype(BF16)
-
-    spread(q_ref, 1, qh_ref, 0)
-    for side, ref in enumerate((k_ref, v_ref)):
-        ext0, ext1, ext2 = ext[3 * side : 3 * side + 3]
-        spread(ref, 1, ext0, BLOCK)
-        spread(ref, 2, ext1, BLOCK)
-        spread(ref, 4, ext2, BLOCK)
-        for head in range(heads):
+            tok[pl.ds(chunk * BLOCK * heads, BLOCK * heads)] = flat(block)
+            for factor, base in ((2, rows), (4, rows * 3 // 2)):
+                part = flat(pooled(block, factor))
+                tok[pl.ds(base * heads + chunk * part.shape[0], part.shape[0])] = part
+        for head in range(heads):
+            for factor, base, target in ((1, 0, ext0), (2, rows, ext1), (4, rows * 3 // 2, ext2)):
+                target[head, pl.ds(BLOCK, rows // factor)] = tok[
+                    pl.ds(base * heads + head, rows // factor, stride=heads)
+                ].astype(BF16)
             near = halo_ref[side, head, :BLOCK]
             level1 = halo_ref[side, head, BLOCK : BLOCK * 3 // 2]
             tmp[:BLOCK] = near.astype(F32)
@@ -132,39 +135,31 @@
         level = jnp.where(is0, 0.0, jnp.where(is1, 1.0, 2.0))
         bias[pair] = jnp.where(ok, level, NEG)
 
-    lane = lax.broadcasted_iota(jnp.int32, (PAIR, width), 1)
+    ones = jnp.ones((columns, width), BF16)
     for pair in range(pairs):
         kind = pair if pair < 2 else 2 + pair % 2
         base2 = pair // 2 * BLOCK
 
-        def one_head(head, stats):
-            def rows_of(side):
-                ext0, ext1, ext2 = ext[3 * side : 3 * side + 3]
-                return jnp.concatenate(
-                    [
-                        ext0[head, pl.ds(PAIR * pair, 3 * BLOCK)],
-                        ext1[head, pl.ds(BLOCK * pair, BLOCK)],
-                        ext2[head, pl.ds(base2, BLOCK)],
-                    ],
-                    0,
-                )
-
+        def rows_of(side, head):
+            ext0, ext1, ext2 = ext[3 * side : 3 * side + 3]
+            return jnp.concatenate(
+                [
+                    ext0[head, pl.ds(PAIR * pair, 3 * BLOCK)],
+                    ext1[head, pl.ds(BLOCK * pair, BLOCK)],
+                    ext2[head, pl.ds(base2, BLOCK)],
+                ],
+                0,
+            )
+
+        for head in range(heads):
             query = qh_ref[head, pl.ds(PAIR * pair, PAIR)]
-            score = lax.dot_general(query, rows_of(0), (((1,), (1,)), ((), ())), preferred_element_type=F32)
+            score = lax.dot_general(query, rows_of(0, head), (((1,), (1,)), ((), ())), preferred_element_type=F32)
             score = score * scale + bias[kind]
             top = jnp.max(score, axis=1, keepdims=True)
-            weight = jnp.exp2(score - top)
-            total = jnp.sum(weight, axis=1, keepdims=True)
-            acc_ref[head, pl.ds(PAIR * pair, PAIR)] = jnp.dot(
-                weight.astype(BF16), rows_of(1), preferred_element_type=F32
-            )
-            stats = jnp.where(lane == head, top, stats)
-            return jnp.where(lane == head + heads, total, stats)
-
-        stats = jnp.zeros((PAIR, width), F32)
-        for head in range(heads):
-            stats = one_head(head, stats)
-        stat_ref[pl.ds(PAIR * pair, PAIR)] = stats
+            weight = jnp.exp2(score - top).astype(BF16)
+            kept = jnp.concatenate([rows_of(1, head), ones], 1)
+            acc_ref[head, pl.ds(PAIR * pair, PAIR)] = jnp.dot(weight, kept, preferred_element_type=F32)
+            top_ref[head, pl.ds(PAIR * pair, PAIR)] = jnp.broadcast_to(top, (PAIR, width))
 
 
 def local(me, queries, keys, values, halo):
@@ -176,71 +171,73 @@
         local_kernel,
         out_shape=(
             jax.ShapeDtypeStruct((heads, rows, width), BF16),
+            jax.ShapeDtypeStruct((heads, rows, 2 * width), F32),
             jax.ShapeDtypeStruct((heads, rows, width), F32),
-            jax.ShapeDtypeStruct((rows, width), F32),
         ),
         in_specs=[SMEM, VMEM, VMEM, VMEM, VMEM],
         out_specs=(VMEM, VMEM, VMEM),
         scratch_shapes=[
-            pltpu.VMEM((rows * heads, width), F32),
+            pltpu.VMEM((rows * 7 // 4 * heads, width), F32),
             pltpu.VMEM((BLOCK * 3 // 2, width), F32),
             pltpu.VMEM((4, PAIR, 5 * BLOCK), F32),
         ]
         + side
         + side,
+        compiler_params=pltpu.CompilerParams(vmem_limit_bytes=28 << 20),
         name="local",
     )(me, queries, keys, values, halo)
 
 
-def far_kernel(sources, me_ref, qh_ref, acc_ref, stat_ref, *refs):
+def far_kernel(sources, me_ref, qh_ref, acc_ref, top_ref, *refs):
     chunks, (out_ref, tok) = refs[:-2], refs[-2:]
-    heads, tile, width = qh_ref.shape
+    heads, rows, width = qh_ref.shape
     count = chunks[0].shape[-2]
     scale = math.log2(math.e) / math.sqrt(width)
     me = me_ref[0]
-    quad = pl.program_id(0) * tile // QUAD
-    limit = me * count + (quad - 1) * (QUAD // 8)
-    columns = count * len(chunks)
-    col = lax.broadcasted_iota(jnp.int32, (1, columns), 1)
-    bias = jnp.full((1, columns), NEG, F32)
-    for at, back in enumerate(sources):
-        ours = (col >= at * count) & (col < (at + 1) * count)
-        number = (me - back) * count + col - at * count
-        ours = ours & (number < limit) & (me >= back)
-        bias = jnp.where(ours, 3.0, bias)
-    for head in range(heads):
-        kept = jnp.concatenate([chunk[0, head] for chunk in chunks], 0)
-        score = lax.dot_general(qh_ref[head], kept, (((1,), (1,)), ((), ())), preferred_element_type=F32)
-        score = score * scale + bias
-        before = stat_ref[:, head : head + 1]
-        top = jnp.maximum(before, jnp.max(score, axis=1, keepdims=True))
-        fade = jnp.exp2(before - top)
-        weight = jnp.exp2(score - top)
-        total = stat_ref[:, heads + head : heads + head + 1] * fade + jnp.sum(weight, axis=1, keepdims=True)
-        kept = jnp.concatenate([chunk[1, head] for chunk in chunks], 0)
-        summed = acc_ref[head] * fade + jnp.dot(weight.astype(BF16), kept, preferred_element_type=F32)
-        tok[pl.ds(head, tile, stride=heads)] = summed * (1.0 / total)
-    out_ref[...] = tok[...].reshape(tile, heads, width).astype(BF16)
-
-
-def far(me, qh, acc, stat, chunks, sources):
+    some = me > 0
+    step = QUAD // 8
+    ones = jnp.ones((count, width), BF16)
+    for quad in range(rows // QUAD):
+        limit = me * count + (quad - 1) * step
+        at = pl.ds(quad * QUAD, QUAD)
+        for head in range(heads):
+            spare = jnp.concatenate([chunks[0][0, head, :step]] * (count // step), 0)
+            far_k, far_v = [], []
+            for chunk, back in zip(chunks, sources):
+                start = (me - back) * count
+                for sub in range(count // step):
+                    good = (start >= 0) & (start + sub * step < limit)
+                    here = pl.ds(sub * step, step)
+                    far_k.append(jnp.where(good, chunk[0, head, here], spare[:step]))
+                    pair = jnp.concatenate([chunk[1, head, here], ones[:step]], 1)
+                    far_v.append(jnp.where(good, pair, jnp.zeros_like(pair)))
+            score = lax.dot_general(
+                qh_ref[head, at], jnp.concatenate(far_k, 0), (((1,), (1,)), ((), ())), preferred_element_type=F32
+            )
+            best = jnp.max(score, axis=1, keepdims=True)
+            best = jnp.where(some, best * scale + 3.0, NEG)
+            before = top_ref[head, at]
+            top = jnp.maximum(before, best)
+            fade = jnp.exp2(before - top)
+            weight = jnp.exp2(score * scale - (top[:, :1] - 3.0)).astype(BF16)
+            summed = jnp.dot(weight, jnp.concatenate(far_v, 0), preferred_element_type=F32)
+            upper = acc_ref[head, at, :width] * fade + summed[:, :width]
+            lower = acc_ref[head, at, width:] * fade + summed[:, width:]
+            tok[pl.ds(quad * QUAD * heads + head, QUAD, stride=heads)] = upper / lower
+        out_ref[at] = tok[pl.ds(quad * QUAD * heads, QUAD * heads)].reshape(QUAD, heads, width).astype(BF16)
+
+
+def far(me, qh, acc, top, chunks, sources):
     heads, rows, width = qh.shape
-    tile = PAIR
     return pl.pallas_call(
         functools.partial(far_kernel, sources),
         out_shape=jax.ShapeDtypeStruct((rows, heads, width), BF16),
-        grid=(rows // tile,),
-        in_specs=[
-            SMEM,
-            pl.BlockSpec((heads, tile, width), lambda i: (0, i, 0)),
-            pl.BlockSpec((heads, tile, width), lambda i: (0, i, 0)),
-            pl.BlockSpec((tile, width), lambda i: (i, 0)),
-        ]
-        + [VMEM] * len(chunks),
-        out_specs=pl.BlockSpec((tile, heads, width), lambda i: (i, 0, 0)),
-        scratch_shapes=[pltpu.VMEM((tile * heads, width), F32)],
+        in_specs=[SMEM, VMEM, VMEM, VMEM] + [VMEM] * len(chunks),
+        out_specs=VMEM,
+        scratch_shapes=[pltpu.VMEM((rows * heads, width), F32)],
+        compiler_params=pltpu.CompilerParams(vmem_limit_bytes=28 << 20),
         name="far",
-    )(me, qh, acc, stat, *chunks)
+    )(me, qh, acc, top, *chunks)
 
 
 def shards(queries, keys, values):

time: 82 us -> 70.5 us (0.86)
  Pallas kernels: 33 us -> 11.6 us
  local copies, waits for them, and re-layouts: 0.69 us -> 6.12 us
  waiting for transfers between devices: 21.6 us -> 26.1 us
    pallas_call x1, Pallas kernels: 16.3 us -> 5.51 us  [far(): pl.pallas_call(functools.partial(far_kernel, sources), out_shape=jax.Shap...]
    pallas_call x1, Pallas kernels: 13.6 us -> 5.45 us  [local(): pl.pallas_call(local_kernel, out_shape=(jax.ShapeDtypeStruct((heads, rows...]
    unnamed x16 -> x10, local copies, waits for them, and re-layouts: 0.69 us -> 6.12 us
    ppermute x8, waiting for transfers between devices: 21.6 us -> 26.1 us  [shifted(): lax.ppermute(value, axis, [(i, i + steps) for i in range(count - steps)])]
    pallas_call x1, Pallas kernels: 3.05 us -> 0.65 us  [prep(): pl.pallas_call(prep_kernel, out_shape=(jax.ShapeDtypeStruct((2, heads, 2...]
  transfers between devices with their start and end apart: 8 -> 8, of which waited for: 2 -> 3; matrix products, arithmetic and copies ran while one was open for 0% -> 0% of each run, Pallas kernels for 17% -> 8%
where the time goes in v2:
time: 70.5 us; the launch traced here: 70.1 us
  starting transfers between devices  26.1 us (37%)
  waiting for transfers between devices  26.1 us (37%)
  Pallas kernels  11.6 us (16%)
  local copies, waits for them, and re-layouts  6.12 us (9%)
    ppermute x8, starting transfers between devices, shifted(): lax.ppermute(value, axis, [(i, i + steps) for i in range(count - steps)])  26.1 us
    ppermute x8, waiting for transfers between devices, shifted(): lax.ppermute(value, axis, [(i, i + steps) for i in range(count - steps)])  26.1 us
    unnamed x10, local copies, waits for them, and re-layouts  6.12 us
    pallas_call x1, Pallas kernels, far(): pl.pallas_call(functools.partial(far_kernel, sources), out_shape=jax.Shap...  5.51 us
    pallas_call x1, Pallas kernels, local(): pl.pallas_call(local_kernel, out_shape=(jax.ShapeDtypeStruct((heads, rows...  5.45 us
  transfers between devices with their start and end apart: 8, of which 3 were waited for; matrix products, arithmetic and copies ran while one was open for 0% of the time, Pallas kernels for 8%

profile of v2, /device:TPU:16, one launch (start us, length us, event | category | flops | bytes accessed | tf_op | source)
XLA Modules:
  0.0 70.1 jit_solution(7205739305201850432)
XLA Ops:
  0.0 0.0 copy-start
  0.0 1.2 %copy-done = bf16[512,8,128]{2,1,0:T(8,128)(2,1)S(1)} copy-done((bf16[512,8,128]{2,1,0:T(8,128)(2,1)S(1)}, bf16[512,8,128]{2,1,0:T(8,128)(2,1)}, u32[]{:S(2)}) %copy-start) | copy-done | bytes 1048600
  1.2 0.0 copy-start.2
  1.2 1.2 %copy-done.2 = bf16[512,8,128]{2,1,0:T(8,128)(2,1)S(1)} copy-done((bf16[512,8,128]{2,1,0:T(8,128)(2,1)S(1)}, bf16[512,8,128]{2,1,0:T(8,128)(2,1)}, u32[]{:S(2)}) %copy-start.2) | copy-done | bytes 1048600
  2.5 0.7 prep.1
  3.1 3.4 %collective-permute-start = (bf16[2,8,128,128]{3,2,1,0:T(8,128)(2,1)S(1)}, bf16[2,8,128,128]{3,2,1,0:T(8,128)(2,1)S(1)}, u32[]{:S(2)}, u32[]{:S(2)}) collective-permute-start(bf16[2,8,128,128]{3,2,1,0:T(8,128)(2,1)S(1)} %get-tuple-element.10), channel_id=1, source_target_pairs={{0,2},{2,4},{4,6},{6,8},{8,10},{10,12},{12,14},{1,3},{3,5},{5,7},{... | collective-permute-start | bytes 1572872 | tf_op jit(solution)/shard_map/ppermute | solution.py:23
  6.5 0.7 collective-permute-start.7
  7.2 0.7 collective-permute-start.6
  7.9 0.7 collective-permute-start.5
  8.6 1.3 %collective-permute-start.4 = (bf16[2,8,64,128]{3,2,1,0:T(8,128)(2,1)S(1)}, bf16[2,8,64,128]{3,2,1,0:T(8,128)(2,1)S(1)}, u32[]{:S(2)}, u32[]{:S(2)}) collective-permute-start(bf16[2,8,64,128]{3,2,1,0:T(8,128)(2,1)S(1)} %get-tuple-element.14), channel_id=1, source_target_pairs={{0,8},{2,10},{4,12},{6,14},{1,9},{3,11},{5,13},{7,15},{16,24},{18,... | collective-permute-start | bytes 786440 | tf_op jit(solution)/shard_map/ppermute | solution.py:23
  9.9 0.0 collective-permute-done.7.refs_6_
  9.9 12.8 %collective-permute-start.3 = (bf16[2,8,64,128]{3,2,1,0:T(8,128)(2,1)S(1)}, bf16[2,8,64,128]{3,2,1,0:T(8,128)(2,1)S(1)}, u32[]{:S(2)}, u32[]{:S(2)}) collective-permute-start(bf16[2,8,64,128]{3,2,1,0:T(8,128)(2,1)S(1)} %get-tuple-element.14), channel_id=1, source_target_pairs={{0,6},{2,8},{4,10},{6,12},{8,14},{1,7},{3,9},{5,11},{7,13},{9,15},... | collective-permute-start | bytes 786440 | tf_op jit(solution)/shard_map/ppermute | solution.py:23
  22.7 0.0 collective-permute-done.6.refs_5_
  22.7 4.7 %collective-permute-start.2 = (bf16[2,8,64,128]{3,2,1,0:T(8,128)(2,1)S(1)}, bf16[2,8,64,128]{3,2,1,0:T(8,128)(2,1)S(1)}, u32[]{:S(2)}, u32[]{:S(2)}) collective-permute-start(bf16[2,8,64,128]{3,2,1,0:T(8,128)(2,1)S(1)} %get-tuple-element.14), channel_id=1, source_target_pairs={{0,4},{2,6},{4,8},{6,10},{8,12},{10,14},{1,5},{3,7},{5,9},{7,11},{... | collective-permute-start | bytes 786440 | tf_op jit(solution)/shard_map/ppermute | solution.py:23
  27.4 15.8 %collective-permute-done.halo_ref = bf16[2,8,128,128]{3,2,1,0:T(8,128)(2,1)S(1)} collective-permute-done((bf16[2,8,128,128]{3,2,1,0:T(8,128)(2,1)S(1)}, bf16[2,8,128,128]{3,2,1,0:T(8,128)(2,1)S(1)}, u32[]{:S(2)}, u32[]{:S(2)}) %collective-permute-start) | collective-permute-done | bytes 524320 | tf_op jit(solution)/shard_map/ppermute | solution.py:23
  43.2 1.9 %collective-permute-start.1 = (bf16[2,8,64,128]{3,2,1,0:T(8,128)(2,1)S(1)}, bf16[2,8,64,128]{3,2,1,0:T(8,128)(2,1)S(1)}, u32[]{:S(2)}, u32[]{:S(2)}) collective-permute-start(bf16[2,8,64,128]{3,2,1,0:T(8,128)(2,1)S(1)} %get-tuple-element.14), channel_id=1, source_target_pairs={{0,2},{2,4},{4,6},{6,8},{8,10},{10,12},{12,14},{1,3},{3,5},{5,7},{... | collective-permute-start | bytes 786440 | tf_op jit(solution)/shard_map/ppermute | solution.py:23
  45.1 0.0 copy-start.1
  45.1 1.2 %copy-done.1 = bf16[512,8,128]{2,1,0:T(8,128)(2,1)S(1)} copy-done((bf16[512,8,128]{2,1,0:T(8,128)(2,1)S(1)}, bf16[512,8,128]{2,1,0:T(8,128)(2,1)}, u32[]{:S(2)}) %copy-start.1) | copy-done | bytes 1048600
  46.3 0.0 copy-start.3
  46.3 1.2 %copy-done.3 = bf16[512,8,128]{2,1,0:T(8,128)(2,1)S(1)} copy-done((bf16[512,8,128]{2,1,0:T(8,128)(2,1)S(1)}, bf16[512,8,128]{2,1,0:T(8,128)(2,1)}, u32[]{:S(2)}) %copy-start.3) | copy-done | bytes 1048600
  47.5 0.0 copy-start.4
  47.5 1.2 %copy-done.4 = bf16[512,8,128]{2,1,0:T(8,128)(2,1)S(1)} copy-done((bf16[512,8,128]{2,1,0:T(8,128)(2,1)S(1)}, bf16[512,8,128]{2,1,0:T(8,128)(2,1)}, u32[]{:S(2)}) %copy-start.4) | copy-done | bytes 1048600
  48.8 5.4 %local.1 = (bf16[8,512,128]{2,1,0:T(8,128)(2,1)S(1)}, f32[8,512,256]{2,1,0:T(8,128)S(1)}, f32[8,512,128]{2,1,0:T(8,128)S(1)}) custom-call(s32[1]{0:T(128)} %bitcast.me_ref, bf16[512,8,128]{2,1,0:T(8,128)(2,1)S(1)} %copy-done.4, bf16[512,8,128]{2,1,0:T(8,128)(2,1)S(1)} %copy-done.1, bf16[512,8,128]{2,1,0:T(8,128)(2,1)S(1)} %copy-done.3, ...), custom_call_target="tpu_custom_call" | custom-call | tf_op jit(solution)/shard_map/local/pallas_call | solution.py:170
  54.2 0.0 collective-permute-done.5.refs_4_
  54.2 0.0 collective-permute-done.4.refs_3_
  54.2 0.0 collective-permute-done.3.refs_2_
  54.2 2.3 %collective-permute-done.2.refs_1_ = bf16[2,8,64,128]{3,2,1,0:T(8,128)(2,1)S(1)} collective-permute-done((bf16[2,8,64,128]{3,2,1,0:T(8,128)(2,1)S(1)}, bf16[2,8,64,128]{3,2,1,0:T(8,128)(2,1)S(1)}, u32[]{:S(2)}, u32[]{:S(2)}) %collective-permute-start.2) | collective-permute-done | bytes 262176 | tf_op jit(solution)/shard_map/ppermute | solution.py:23
  56.6 8.0 %collective-permute-done.1.refs_0_ = bf16[2,8,64,128]{3,2,1,0:T(8,128)(2,1)S(1)} collective-permute-done((bf16[2,8,64,128]{3,2,1,0:T(8,128)(2,1)S(1)}, bf16[2,8,64,128]{3,2,1,0:T(8,128)(2,1)S(1)}, u32[]{:S(2)}, u32[]{:S(2)}) %collective-permute-start.1) | collective-permute-done | bytes 262176 | tf_op jit(solution)/shard_map/ppermute | solution.py:23
  64.5 5.5 %far.1 = bf16[512,8,128]{2,1,0:T(8,128)(2,1)} custom-call(s32[1]{0:T(128)} %bitcast.me_ref, bf16[8,512,128]{2,1,0:T(8,128)(2,1)S(1)} %get-tuple-element.11.qh_ref, f32[8,512,256]{2,1,0:T(8,128)S(1)} %get-tuple-element.12.acc_ref, f32[8,512,128]{2,1,0:T(8,128)S(1)} %get-tuple-element.13.top_ref, bf16[2,8,64,128]{3,2,1,0:T(8,128)(2,1)S(1)} %collective-permute-done.1.refs_0_, ...), custom_call_target="tpu_custom_call" | custom-call | tf_op jit(solution)/shard_map/far/pallas_call | solution.py:232
Async XLA Ops:
  0.0 1.2 %copy-start = (bf16[512,8,128]{2,1,0:T(8,128)(2,1)S(1)}, bf16[512,8,128]{2,1,0:T(8,128)(2,1)}, u32[]{:S(2)}) copy-start(bf16[512,8,128]{2,1,0:T(8,128)(2,1)} %k_ref.3) | copy-start | bytes 3145732
  1.2 1.2 %copy-start.2 = (bf16[512,8,128]{2,1,0:T(8,128)(2,1)S(1)}, bf16[512,8,128]{2,1,0:T(8,128)(2,1)}, u32[]{:S(2)}) copy-start(bf16[512,8,128]{2,1,0:T(8,128)(2,1)} %v_ref.3) | copy-start | bytes 3145732
  3.1 40.1 %collective-permute-start = (bf16[2,8,128,128]{3,2,1,0:T(8,128)(2,1)S(1)}, bf16[2,8,128,128]{3,2,1,0:T(8,128)(2,1)S(1)}, u32[]{:S(2)}, u32[]{:S(2)}) collective-permute-start(bf16[2,8,128,128]{3,2,1,0:T(8,128)(2,1)S(1)} %get-tuple-element.10), channel_id=1, source_target_pairs={{0,2},{2,4},{4,6},{6,8},{8,10},{10,12},{12,14},{1,3},{3,5},{5,7},{... | collective-permute-start | bytes 1572872 | tf_op jit(solution)/shard_map/ppermute | solution.py:23
  6.5 3.4 %collective-permute-start.7 = (bf16[2,8,64,128]{3,2,1,0:T(8,128)(2,1)S(1)}, bf16[2,8,64,128]{3,2,1,0:T(8,128)(2,1)S(1)}, u32[]{:S(2)}, u32[]{:S(2)}) collective-permute-start(bf16[2,8,64,128]{3,2,1,0:T(8,128)(2,1)S(1)} %get-tuple-element.14), channel_id=1, source_target_pairs={{0,14},{1,15},{16,30},{17,31}} | collective-permute-start | bytes 786440 | tf_op jit(solution)/shard_map/ppermute | solution.py:23
  7.2 15.5 %collective-permute-start.6 = (bf16[2,8,64,128]{3,2,1,0:T(8,128)(2,1)S(1)}, bf16[2,8,64,128]{3,2,1,0:T(8,128)(2,1)S(1)}, u32[]{:S(2)}, u32[]{:S(2)}) collective-permute-start(bf16[2,8,64,128]{3,2,1,0:T(8,128)(2,1)S(1)} %get-tuple-element.14), channel_id=1, source_target_pairs={{0,12},{2,14},{1,13},{3,15},{16,28},{18,30},{17,29},{19,31}} | collective-permute-start | bytes 786440 | tf_op jit(solution)/shard_map/ppermute | solution.py:23
  7.9 46.3 %collective-permute-start.5 = (bf16[2,8,64,128]{3,2,1,0:T(8,128)(2,1)S(1)}, bf16[2,8,64,128]{3,2,1,0:T(8,128)(2,1)S(1)}, u32[]{:S(2)}, u32[]{:S(2)}) collective-permute-start(bf16[2,8,64,128]{3,2,1,0:T(8,128)(2,1)S(1)} %get-tuple-element.14), channel_id=1, source_target_pairs={{0,10},{2,12},{4,14},{1,11},{3,13},{5,15},{16,26},{18,28},{20,30},... | collective-permute-start | bytes 786440 | tf_op jit(solution)/shard_map/ppermute | solution.py:23
  8.6 45.7 %collective-permute-start.4 = (bf16[2,8,64,128]{3,2,1,0:T(8,128)(2,1)S(1)}, bf16[2,8,64,128]{3,2,1,0:T(8,128)(2,1)S(1)}, u32[]{:S(2)}, u32[]{:S(2)}) collective-permute-start(bf16[2,8,64,128]{3,2,1,0:T(8,128)(2,1)S(1)} %get-tuple-element.14), channel_id=1, source_target_pairs={{0,8},{2,10},{4,12},{6,14},{1,9},{3,11},{5,13},{7,15},{16,24},{18,... | collective-permute-start | bytes 786440 | tf_op jit(solution)/shard_map/ppermute | solution.py:23
  9.9 44.4 %collective-permute-start.3 = (bf16[2,8,64,128]{3,2,1,0:T(8,128)(2,1)S(1)}, bf16[2,8,64,128]{3,2,1,0:T(8,128)(2,1)S(1)}, u32[]{:S(2)}, u32[]{:S(2)}) collective-permute-start(bf16[2,8,64,128]{3,2,1,0:T(8,128)(2,1)S(1)} %get-tuple-element.14), channel_id=1, source_target_pairs={{0,6},{2,8},{4,10},{6,12},{8,14},{1,7},{3,9},{5,11},{7,13},{9,15},... | collective-permute-start | bytes 786440 | tf_op jit(solution)/shard_map/ppermute | solution.py:23
  22.7 33.8 %collective-permute-start.2 = (bf16[2,8,64,128]{3,2,1,0:T(8,128)(2,1)S(1)}, bf16[2,8,64,128]{3,2,1,0:T(8,128)(2,1)S(1)}, u32[]{:S(2)}, u32[]{:S(2)}) collective-permute-start(bf16[2,8,64,128]{3,2,1,0:T(8,128)(2,1)S(1)} %get-tuple-element.14), channel_id=1, source_target_pairs={{0,4},{2,6},{4,8},{6,10},{8,12},{10,14},{1,5},{3,7},{5,9},{7,11},{... | collective-permute-start | bytes 786440 | tf_op jit(solution)/shard_map/ppermute | solution.py:23
  43.2 21.4 %collective-permute-start.1 = (bf16[2,8,64,128]{3,2,1,0:T(8,128)(2,1)S(1)}, bf16[2,8,64,128]{3,2,1,0:T(8,128)(2,1)S(1)}, u32[]{:S(2)}, u32[]{:S(2)}) collective-permute-start(bf16[2,8,64,128]{3,2,1,0:T(8,128)(2,1)S(1)} %get-tuple-element.14), channel_id=1, source_target_pairs={{0,2},{2,4},{4,6},{6,8},{8,10},{10,12},{12,14},{1,3},{3,5},{5,7},{... | collective-permute-start | bytes 786440 | tf_op jit(solution)/shard_map/ppermute | solution.py:23
  45.1 1.2 %copy-start.1 = (bf16[512,8,128]{2,1,0:T(8,128)(2,1)S(1)}, bf16[512,8,128]{2,1,0:T(8,128)(2,1)}, u32[]{:S(2)}) copy-start(bf16[512,8,128]{2,1,0:T(8,128)(2,1)} %k_ref.3) | copy-start | bytes 3145732
  46.3 1.2 %copy-start.3 = (bf16[512,8,128]{2,1,0:T(8,128)(2,1)S(1)}, bf16[512,8,128]{2,1,0:T(8,128)(2,1)}, u32[]{:S(2)}) copy-start(bf16[512,8,128]{2,1,0:T(8,128)(2,1)} %v_ref.3) | copy-start | bytes 3145732
  47.5 1.2 %copy-start.4 = (bf16[512,8,128]{2,1,0:T(8,128)(2,1)S(1)}, bf16[512,8,128]{2,1,0:T(8,128)(2,1)}, u32[]{:S(2)}) copy-start(bf16[512,8,128]{2,1,0:T(8,128)(2,1)} %q_ref.1) | copy-start | bytes 3145732
